TPU v7x, 512 devices: a whole 4x4x16 slice. The times are simulated.
512 devices in a mesh: seq: 128 (over z, y, core), head: 4 (over x).
Axes of the slice: x: 4, y: 4, z: 16, core: 2. Of those that a mesh axis runs over, the one named last changes fastest.
Arguments:
- query_states: float32 [32768, 2048], P('seq', 'head'), may hold values from -6.4 to 6.4
- key_states: float32 [32768, 2048], P('seq', 'head'), may hold values from -6.4 to 6.4
- value_states: float32 [32768, 2048], P('seq', 'head'), may hold values from -30 to 30
- out_cotangent: float32 [32768, 2048], P('seq', 'head'), may hold values from -20 to 20
- norm_gain: float32 [2048], P('head'), may hold values from 0.5 to 1.5
- norm_bias: float32 [2048], P('head'), may hold values from -3 to 3
Outputs:
- normed: float32 [32768, 2048], P('seq', 'head')
- query_grad: float32 [32768, 2048], P('seq', 'head')
- key_grad: float32 [32768, 2048], P('seq', 'head')
- value_grad: float32 [32768, 2048], P('seq', 'head')
All inputs are finite; a program needn't handle non-finite values.
Results may differ from a plain program's by a relative error of at most 0.0003.
Values sent between devices are 32-bit elements; how exact they have to be, the bound alone decides.
No kernel may reach another device: no remote copies, remote signals or barrier semaphores. Data moves between devices by JAX's collectives and lax.ppermute only.
A program may use at most 64 MiB of HBM per device.

v0:
```python
import functools
import math

import jax
import jax.numpy as jnp
from jax import lax
from jax.experimental import pallas as pl
from jax.experimental.pallas import tpu as pltpu
from jax.sharding import PartitionSpec as P

D = 2048
HEADS = 16
BLK = 128
EPS = 1e-05
HD = D // HEADS
INV_ROOT = 1.0 / math.sqrt(HD)
LOG2E = 1.0 / math.log(2.0)

L45 = ((16, 4), (16, 5))
GATHERED = ((64, 2),) + L45 + ((32, 3),) + L45 + ((32, 3),) + L45 + L45
NEAR = 256
OWN = 256
PEER = 384
KEYS = NEAR + OWN + PEER
LEVELS = ((NEAR, 0),) + GATHERED + ((128, 1),) + GATHERED

VM = pl.BlockSpec(memory_space=pltpu.VMEM)
SM = pl.BlockSpec(memory_space=pltpu.SMEM)
F32 = jnp.float32
BF16 = jnp.bfloat16


def shape(*dims):
    return jax.ShapeDtypeStruct(dims, F32)


def call(body, out, args, name, scalars=0, scratch=()):
    return pl.pallas_call(
        body,
        out_shape=out,
        in_specs=[SM] * scalars + [VM] * (len(args) - scalars),
        out_specs=jax.tree.map(lambda _: VM, out),
        scratch_shapes=scratch,
        name=name,
    )(*args)


def halves(value, buf):
    rows = value.shape[0] // 2
    buf[...] = value
    return 0.5 * (buf[pl.ds(0, rows, stride=2), :] + buf[pl.ds(1, rows, stride=2), :])


def doubled(value, buf):
    rows = value.shape[0]
    half = 0.5 * value
    buf[pl.ds(0, rows, stride=2), :] = half
    buf[pl.ds(1, rows, stride=2), :] = half
    return buf[...]


def buffers(count, *rows):
    return [pltpu.VMEM((count, n, HD), F32) for n in rows]


def coarsen_body(k_ref, v_ref, l1, l2, l3, l4, b0, b1, b2, b3):
    for h in range(8):
        src = k_ref if h < 4 else v_ref
        col = slice((h % 4) * HD, (h % 4 + 1) * HD)
        to = slice(h * HD, (h + 1) * HD)
        one = halves(src[:, col], b0.at[h])
        l1[:, to] = one
        two = halves(one, b1.at[h])
        l2[:, to] = two
        three = halves(two, b2.at[h])
        l3[:, to] = three
        four = halves(three, b3.at[h])
        for j in range(4):
            l4[j, :, to] = four


def route_body(zpos, z_in, l3, c0, y23, buf):
    z = zpos[0]
    c0[0:16, :] = z_in[z ^ 1]
    for h in range(8):
        to = slice(h * HD, (h + 1) * HD)
        for j in (2, 3):
            c0[8 * j : 8 * j + 8, to] = halves(z_in[z ^ j, :, to], buf.at[2 * h + j - 2])
    y23[0:32, :] = l3[...]
    y23[32:64, :] = c0[...]


def pack_body(*refs):
    out = refs[-1]
    row = 0
    for ref in refs[:-1]:
        out[row : row + ref.shape[0], :] = ref[...]
        row += ref.shape[0]


def split2(x):
    hi = x.astype(BF16)
    return hi, (x - hi.astype(F32)).astype(BF16)


def split3(x):
    hi = x.astype(BF16)
    rest = x - hi.astype(F32)
    mid = rest.astype(BF16)
    return hi, mid, (rest - mid.astype(F32)).astype(BF16)


NT = (((1,), (1,)), ((), ()))
NN = (((1,), (0,)), ((), ()))
TN = (((0,), (0,)), ((), ()))


def dot(a, b, dims):
    return lax.dot_general(a, b, dims, preferred_element_type=F32)


def cat(*parts):
    return jnp.concatenate(parts, axis=1)


def scores(keys, query):
    kh, km, kl = split3(keys)
    qh, qm, ql = split3(query)
    key2 = cat(kh, km)
    return dot(key2, cat(qh, qh), NT) + (dot(key2, cat(qm, qm), NT) + dot(cat(kh, kl), cat(ql, qh), NT))


def dot_nt(a, b):
    ah, al = split2(a)
    bh, bl = split2(b)
    return dot(cat(ah, al), cat(bh, bh), NT) + dot(ah, bl, NT)


def dot_nn(ah, al, b):
    bh, bl = split2(b)
    both = dot(ah, cat(bh, bl), NN)
    half = b.shape[1]
    return both[:, :half] + both[:, half:] + dot(al, bh, NN)


def dot_tn(a, bh, bl):
    ah, al = split2(a)
    return dot(ah, bh, TN) + (dot(ah, bl, TN) + dot(al, bh, TN))


def head_cols(h):
    return slice(h * HD, (h + 1) * HD)


def forward_body(q_ref, k_ref, v_ref, own, peer, ct, gain, p_out, att, send):
    for h in range(4):
        at = head_cols(h)
        query = q_ref[:, at] * (INV_ROOT * LOG2E)
        vat = head_cols(4 + h)
        blocks = (
            scores(k_ref[:, at], query),
            scores(own[128:384, at], query),
            scores(peer[:, at], query),
        )
        s = jnp.concatenate(blocks, axis=0)
        parts = []
        row = 0
        for rows, level in LEVELS:
            seg = s[row : row + rows]
            parts.append(seg + float(level) if level else seg)
            row += rows
        s = jnp.concatenate(parts, axis=0)
        top = jnp.max(s, axis=0, keepdims=True)
        e = jnp.exp2(s - top)
        p = e * (1.0 / jnp.sum(e, axis=0, keepdims=True))
        p_out[h] = p
        values = jnp.concatenate((v_ref[:, at], own[128:384, vat], peer[:, vat]), axis=0)
        ph, pl_ = split2(p)
        att[:, at] = dot_tn(values, ph, pl_).T
    a = att[...]
    width = 4 * HD
    total = jnp.sum(a, axis=1, keepdims=True)
    mean = total * (1.0 / width)
    away = a - mean
    sg = ct[...] * gain[...]
    lane = lax.broadcasted_iota(jnp.int32, (NEAR, HD), 1)
    stats = jnp.where(lane == 0, mean, 0.0)
    for j, value in (
        (1, jnp.sum(away * away, axis=1, keepdims=True)),
        (2, jnp.sum(sg, axis=1, keepdims=True)),
        (3, jnp.sum(sg * away, axis=1, keepdims=True)),
    ):
        stats = jnp.where(lane == j, value, stats)
    rows = stats.T[0:8]
    for j in range(4):
        send[j] = rows


def backward_body(
    q_ref, k_ref, v_ref, own, peer, ct, gain, bias, p_in, att, got,
    normed, dq, dk, dv, d_own, d_peer,
):
    stat = [got[j] for j in range(4)]
    mean = (stat[0][0:1] + stat[1][0:1] + stat[2][0:1] + stat[3][0:1]) * 0.25
    square = jnp.zeros_like(mean)
    total = jnp.zeros_like(mean)
    cross = jnp.zeros_like(mean)
    for part in stat:
        shift = part[0:1] - mean
        square = square + (part[1:2] + (4.0 * HD) * (shift * shift))
        total = total + part[2:3]
        cross = cross + (part[3:4] + part[2:3] * shift)
    inv = lax.rsqrt(square * (1.0 / D) + EPS)
    cross = cross * inv
    sub = lax.broadcasted_iota(jnp.int32, (HD, NEAR), 0)
    table = jnp.where(sub == 0, mean, 0.0)
    for j, value in ((1, inv), (2, total * (1.0 / D)), (3, cross * (1.0 / D))):
        table = jnp.where(sub == j, value, table)
    cols = table.T
    mean, inv, total, cross = (cols[:, j : j + 1] for j in range(4))
    for h in range(4):
        at = head_cols(h)
        vat = head_cols(4 + h)
        hat = (att[:, at] - mean) * inv
        normed[:, at] = hat * gain[:, at] + bias[:, at]
        g = inv * (ct[:, at] * gain[:, at] - total - hat * cross)
        p = p_in[h]
        values = jnp.concatenate((v_ref[:, at], own[128:384, vat], peer[:, vat]), axis=0)
        keys = jnp.concatenate((k_ref[:, at], own[128:384, at], peer[:, at]), axis=0)
        dp = dot_nt(values, g * INV_ROOT)
        ph, pl_ = split2(p)
        dval = dot_nn(ph, pl_, g)
        ds = p * (dp - jnp.sum(p * dp, axis=0, keepdims=True))
        sh, sl = split2(ds)
        dkey = dot_nn(sh, sl, q_ref[:, at])
        dq[:, at] = dot_tn(keys, sh, sl).T
        dk[:, at] = dkey[0:256]
        dv[:, at] = dval[0:256]
        d_own[:, at] = dkey[256:512]
        d_own[:, vat] = dval[256:512]
        d_peer[:, at] = dkey[512:896]
        d_peer[:, vat] = dval[512:896]


def sum_body(d_own, got, c1a, c1b, c2, c3, c0):
    row = 0
    for ref in (c1a, c1b, c2, c3, c0):
        n = ref.shape[0]
        ref[...] = d_own[row : row + n, :] + got[128 + row : 128 + row + n, :]
        row += n


def unroute_body(zpos, c0, y1, y2, y3, send, buf):
    z = zpos[0]
    g = c0[...] + y1[...] + (y2[32:64, :] + y3[32:64, :])
    send[z] = jnp.zeros((16, 8 * HD), F32)
    send[z ^ 1] = g[0:16]
    for j in (2, 3):
        for h in range(8):
            to = slice(h * HD, (h + 1) * HD)
            send[z ^ j, :, to] = doubled(g[8 * j : 8 * j + 8, to], buf.at[2 * h + j - 2])


def finish_body(zpos, dk0, dv0, got, y1a, y2, y3, z_in, dk, dv, s3, s2, s1, s0):
    z = zpos[0]
    for h in range(8):
        to = slice(h * HD, (h + 1) * HD)
        part = z_in[z ^ 1, :, to] + (z_in[z ^ 2, :, to] + z_in[z ^ 3, :, to])
        part = doubled(part, s3.at[h]) + (y2[0:32, to] + y3[0:32, to])
        part = doubled(part, s2.at[h]) + y1a[:, to]
        part = doubled(part, s1.at[h]) + got[0:128, to]
        src, dst = (dk0, dk) if h < 4 else (dv0, dv)
        col = slice((h % 4) * HD, (h % 4 + 1) * HD)
        dst[:, col] = src[:, col] + doubled(part, s0.at[h])


def body(query, key, value, cotangent, gain, bias):
    seq = lax.axis_size("seq")
    zpos = (lax.axis_index("seq") // 8 % 4).reshape(1).astype(jnp.int32)
    z_groups = [[zh * 32 + zl * 8 + r for zl in range(4)] for zh in range(seq // 32) for r in range(8)]

    def swap(x, mask):
        return lax.ppermute(x, "seq", [(i, i ^ mask) for i in range(seq)])

    def z_swap(x):
        return lax.all_to_all(x, "seq", 0, 0, axis_index_groups=z_groups, tiled=True)

    gain = gain.reshape(1, -1)
    bias = bias.reshape(1, -1)
    l1, l2, l3, l4 = call(
        coarsen_body,
        (shape(128, 1024), shape(64, 1024), shape(32, 1024), shape(4, 16, 1024)),
        (key, value),
        "coarsen",
        0,
        buffers(8, 256, 128, 64, 32),
    )
    c1a = swap(l2, 2)
    z_in = z_swap(l4)
    c0, y23 = call(route_body, (shape(32, 1024), shape(64, 1024)), (zpos, z_in, l3), "route", 1, buffers(16, 16))
    c1b = swap(c0, 2)
    c2 = swap(y23, 4)
    c3 = swap(y23, 6)
    own = call(pack_body, shape(384, 1024), (l1, c1a, c1b, c2, c3, c0), "pack")
    peer = swap(own, 1)
    p, att, send = call(
        forward_body,
        (shape(4, KEYS, NEAR), shape(256, 512), shape(4, 8, 256)),
        (query, key, value, own, peer, cotangent, gain),
        "forward",
    )
    got = lax.all_to_all(send, "head", 0, 0, tiled=True)
    normed, dq, dk0, dv0, d_own, d_peer = call(
        backward_body,
        (shape(256, 512),) * 4 + (shape(256, 1024), shape(384, 1024)),
        (query, key, value, own, peer, cotangent, gain, bias, p, att, got),
        "backward",
    )
    d_got = swap(d_peer, 1)
    g1a, g1b, g2, g3, g0 = call(
        sum_body,
        (shape(64, 1024), shape(32, 1024), shape(64, 1024), shape(64, 1024), shape(32, 1024)),
        (d_own, d_got),
        "add_peer",
    )
    r1b = swap(g1b, 2)
    r2 = swap(g2, 4)
    r3 = swap(g3, 6)
    r1a = swap(g1a, 2)
    z_send = call(unroute_body, shape(4, 16, 1024), (zpos, g0, r1b, r2, r3), "unroute", 1, buffers(16, 16))
    z_got = z_swap(z_send)
    dk, dv = call(
        finish_body,
        (shape(256, 512), shape(256, 512)),
        (zpos, dk0, dv0, d_got, r1a, r2, r3, z_got),
        "finish",
        1,
        buffers(8, 32, 64, 128, 256),
    )
    return normed, dq, dk, dv


def solution(mesh):
    both = P("seq", "head")
    return jax.shard_map(
        body,
        mesh=mesh,
        in_specs=(both,) * 4 + (P("head"),) * 2,
        out_specs=(both,) * 4,
        check_vma=False,
    )
```

profile of v0, /device:TPU:1, one launch (start us, length us, event | category | flops | bytes accessed | tf_op | source)
XLA Modules:
  0.0 123.0 jit_solution(7361924810840631733)
XLA Ops:
  0.6 2.5 %coarsen.1 = (f32[128,1024]{1,0:T(8,128)}, f32[64,1024]{1,0:T(8,128)}, f32[32,1024]{1,0:T(8,128)}, f32[4,16,1024]{2,1,0:T(8,128)}) custom-call(f32[256,512]{1,0:T(8,128)} %k_ref.5, f32[256,512]{1,0:T(8,128)} %v_ref.5), custom_call_target="tpu_custom_call" | custom-call | tf_op jit(solution)/shard_map/coarsen/pallas_call | solution.py:38
  3.1 6.4 %all-to-all-start = ((f32[4,16,1024]{2,1,0:T(8,128)}), f32[4,16,1024]{2,1,0:T(8,128)S(1)}, u32[]{:S(2)}, u32[]{:S(2)}) async-start(f32[4,16,1024]{2,1,0:T(8,128)} %get-tuple-element.28), calls=%async_computation | async-start | bytes 524288 | tf_op jit(solution)/shard_map/all_to_all | solution.py:286
  9.5 3.2 %collective-permute-start = (f32[64,1024]{1,0:T(8,128)}, f32[64,1024]{1,0:T(8,128)S(1)}, u32[]{:S(2)}, u32[]{:S(2)}) collective-permute-start(f32[64,1024]{1,0:T(8,128)} %get-tuple-element.27), channel_id=1, source_target_pairs={{0,8},{4,12},{8,0},{12,4},{16,24},{20,28},{24,16},{28,20},{32,40},... | collective-permute-start | bytes 786440 | tf_op jit(solution)/shard_map/ppermute | solution.py:283
  12.8 2.4 %all-to-all-done.z_in = f32[4,16,1024]{2,1,0:T(8,128)S(1)} async-done(((f32[4,16,1024]{2,1,0:T(8,128)}), f32[4,16,1024]{2,1,0:T(8,128)S(1)}, u32[]{:S(2)}, u32[]{:S(2)}) %all-to-all-start) | async-done | bytes 262176 | tf_op jit(solution)/shard_map/all_to_all | solution.py:286
  15.2 0.0 copy-start.2
  15.2 0.7 copy-done.2
  15.9 1.8 %route.1 = (f32[32,1024]{1,0:T(8,128)}, f32[64,1024]{1,0:T(8,128)}) custom-call(s32[1]{0:T(128)} %bitcast.zpos, f32[4,16,1024]{2,1,0:T(8,128)} %copy-done.2, f32[32,1024]{1,0:T(8,128)} %get-tuple-element.29.l3), custom_call_target="tpu_custom_call" | custom-call | tf_op jit(solution)/shard_map/route/pallas_call | solution.py:38
  17.6 6.6 %collective-permute-start.3 = (f32[64,1024]{1,0:T(8,128)}, f32[64,1024]{1,0:T(8,128)S(1)}, u32[]{:S(2)}, u32[]{:S(2)}) collective-permute-start(f32[64,1024]{1,0:T(8,128)} %get-tuple-element.31), channel_id=1, source_target_pairs={{0,24},{4,28},{8,16},{12,20},{16,8},{20,12},{24,0},{28,4},{32,56},... | collective-permute-start | bytes 786440 | tf_op jit(solution)/shard_map/ppermute | solution.py:283
  24.2 2.3 %collective-permute-start.2 = (f32[64,1024]{1,0:T(8,128)}, f32[64,1024]{1,0:T(8,128)S(1)}, u32[]{:S(2)}, u32[]{:S(2)}) collective-permute-start(f32[64,1024]{1,0:T(8,128)} %get-tuple-element.31), channel_id=1, source_target_pairs={{0,16},{4,20},{8,24},{12,28},{16,0},{20,4},{24,8},{28,12},{32,48},... | collective-permute-start | bytes 786440 | tf_op jit(solution)/shard_map/ppermute | solution.py:283
  26.5 2.1 %collective-permute-start.1 = (f32[32,1024]{1,0:T(8,128)}, f32[32,1024]{1,0:T(8,128)S(1)}, u32[]{:S(2)}, u32[]{:S(2)}) collective-permute-start(f32[32,1024]{1,0:T(8,128)} %get-tuple-element.30.refs_5_), channel_id=1, source_target_pairs={{0,8},{4,12},{8,0},{12,4},{16,24},{20,28},{24,16},{28,20},{32,40},... | collective-permute-start | bytes 393224 | tf_op jit(solution)/shard_map/ppermute | solution.py:283
  28.6 0.0 collective-permute-done.refs_1_
  28.6 0.0 copy-start.6
  28.7 4.9 %collective-permute-done.1.refs_2_ = f32[32,1024]{1,0:T(8,128)S(1)} collective-permute-done((f32[32,1024]{1,0:T(8,128)}, f32[32,1024]{1,0:T(8,128)S(1)}, u32[]{:S(2)}, u32[]{:S(2)}) %collective-permute-start.1) | collective-permute-done | bytes 131104 | tf_op jit(solution)/shard_map/ppermute | solution.py:283
  33.6 0.0 copy-start.10
  33.6 0.0 collective-permute-done.3.refs_4_
  33.6 0.0 copy-start.7
  33.6 0.0 collective-permute-done.2.refs_3_
  33.6 0.0 copy-start.8
  33.6 0.0 copy-done.6
  33.6 0.6 copy-done.10
  34.2 0.1 copy-done.7
  34.3 0.1 copy-done.8
  34.4 2.6 %pack.1.own = f32[384,1024]{1,0:T(8,128)} custom-call(f32[128,1024]{1,0:T(8,128)} %get-tuple-element.26.refs_0_, f32[64,1024]{1,0:T(8,128)} %copy-done.6, f32[32,1024]{1,0:T(8,128)} %copy-done.10, f32[64,1024]{1,0:T(8,128)} %copy-done.8, f32[64,1024]{1,0:T(8,128)} %copy-done.7, f32[32,1024]{1,0:T(8,128)} %get-tuple-element.30.refs_5_), custom_call_target="tpu_custom_call" | custom-call | tf_op jit(solution)/shard_map/pack/pallas_call | solution.py:38
  37.0 6.2 %collective-permute-start.4 = (f32[384,1024]{1,0:T(8,128)}, f32[384,1024]{1,0:T(8,128)S(1)}, u32[]{:S(2)}, u32[]{:S(2)}) collective-permute-start(f32[384,1024]{1,0:T(8,128)} %pack.1.own), channel_id=1, source_target_pairs={{0,4},{4,0},{8,12},{12,8},{16,20},{20,16},{24,28},{28,24},{32,36},... | collective-permute-start | bytes 4718600 | tf_op jit(solution)/shard_map/ppermute | solution.py:283
  43.2 3.2 %collective-permute-done.4.peer = f32[384,1024]{1,0:T(8,128)S(1)} collective-permute-done((f32[384,1024]{1,0:T(8,128)}, f32[384,1024]{1,0:T(8,128)S(1)}, u32[]{:S(2)}, u32[]{:S(2)}) %collective-permute-start.4) | collective-permute-done | bytes 1572896 | tf_op jit(solution)/shard_map/ppermute | solution.py:283
  46.4 0.0 copy-start.1
  46.4 1.2 copy-done.1
  47.6 9.0 %forward.1 = (f32[4,896,256]{2,1,0:T(8,128)}, f32[256,512]{1,0:T(8,128)}, f32[4,8,256]{2,1,0:T(8,128)}) custom-call(f32[256,512]{1,0:T(8,128)} %q_ref.3, f32[256,512]{1,0:T(8,128)} %k_ref.5, f32[256,512]{1,0:T(8,128)} %v_ref.5, f32[384,1024]{1,0:T(8,128)} %pack.1.own, f32[384,1024]{1,0:T(8,128)} %copy-done.1, f32[256,512]{1,0:T(8,128)} %ct.3, f32[1,512]{1,0:T(1,128)} %bitcast.3), custom_call_target="tpu_custom_call" | custom-call | tf_op jit(solution)/shard_map/forward/pallas_call | solution.py:38
  56.6 8.4 %all_to_all.15.got = f32[4,8,256]{2,1,0:T(8,128)} all-to-all(f32[4,8,256]{2,1,0:T(8,128)} %get-tuple-element.34), channel_id=1, replica_groups=mesh['seq'=128,'head'=4] {'head'}, dimensions={0} | all-to-all | bytes 65536 | tf_op jit(solution)/shard_map/all_to_all | solution.py:312
  65.0 10.4 %backward.1 = (f32[256,512]{1,0:T(8,128)}, f32[256,512]{1,0:T(8,128)}, f32[256,512]{1,0:T(8,128)}, f32[256,512]{1,0:T(8,128)}, f32[256,1024]{1,0:T(8,128)}, /*index=5*/f32[384,1024]{1,0:T(8,128)}) custom-call(f32[256,512]{1,0:T(8,128)} %q_ref.3, f32[256,512]{1,0:T(8,128)} %k_ref.5, f32[256,512]{1,0:T(8,128)} %v_ref.5, f32[384,1024]{1,0:T(8,128)} %pack.1.own, ...), custom_call_target="tpu_custom_call" | custom-call | tf_op jit(solution)/shard_map/backward/pallas_call | solution.py:38
  75.5 3.7 %collective-permute-start.5 = (f32[384,1024]{1,0:T(8,128)}, f32[384,1024]{1,0:T(8,128)S(1)}, u32[]{:S(2)}, u32[]{:S(2)}) collective-permute-start(f32[384,1024]{1,0:T(8,128)} %get-tuple-element.39), channel_id=1, source_target_pairs={{0,4},{4,0},{8,12},{12,8},{16,20},{20,16},{24,28},{28,24},{32,36},... | collective-permute-start | bytes 4718600 | tf_op jit(solution)/shard_map/ppermute | solution.py:283
  79.2 3.2 %collective-permute-done.5.got = f32[384,1024]{1,0:T(8,128)S(1)} collective-permute-done((f32[384,1024]{1,0:T(8,128)}, f32[384,1024]{1,0:T(8,128)S(1)}, u32[]{:S(2)}, u32[]{:S(2)}) %collective-permute-start.5) | collective-permute-done | bytes 1572896 | tf_op jit(solution)/shard_map/ppermute | solution.py:283
  82.4 0.0 copy-start
  82.4 1.2 copy-done
  83.6 2.7 %add_peer.1 = (f32[64,1024]{1,0:T(8,128)}, f32[32,1024]{1,0:T(8,128)}, f32[64,1024]{1,0:T(8,128)}, f32[64,1024]{1,0:T(8,128)}, f32[32,1024]{1,0:T(8,128)}) custom-call(f32[256,1024]{1,0:T(8,128)} %get-tuple-element.40.d_own, f32[384,1024]{1,0:T(8,128)} %copy-done), custom_call_target="tpu_custom_call" | custom-call | tf_op jit(solution)/shard_map/add_peer/pallas_call | solution.py:38
  86.3 0.0 copy-start.12
  86.3 4.1 %collective-permute-start.7 = (f32[64,1024]{1,0:T(8,128)}, f32[64,1024]{1,0:T(8,128)S(1)}, u32[]{:S(2)}, u32[]{:S(2)}) collective-permute-start(f32[64,1024]{1,0:T(8,128)} %get-tuple-element.42), channel_id=1, source_target_pairs={{0,16},{4,20},{8,24},{12,28},{16,0},{20,4},{24,8},{28,12},{32,48},... | collective-permute-start | bytes 786440 | tf_op jit(solution)/shard_map/ppermute | solution.py:283
  90.4 2.6 %collective-permute-start.8 = (f32[64,1024]{1,0:T(8,128)}, f32[64,1024]{1,0:T(8,128)S(1)}, u32[]{:S(2)}, u32[]{:S(2)}) collective-permute-start(f32[64,1024]{1,0:T(8,128)} %get-tuple-element.43), channel_id=1, source_target_pairs={{0,24},{4,28},{8,16},{12,20},{16,8},{20,12},{24,0},{28,4},{32,56},... | collective-permute-start | bytes 786440 | tf_op jit(solution)/shard_map/ppermute | solution.py:283
  93.0 1.9 %collective-permute-start.9 = (f32[32,1024]{1,0:T(8,128)}, f32[32,1024]{1,0:T(8,128)S(1)}, u32[]{:S(2)}, u32[]{:S(2)}) collective-permute-start(f32[32,1024]{1,0:T(8,128)} %get-tuple-element.45), channel_id=1, source_target_pairs={{0,8},{4,12},{8,0},{12,4},{16,24},{20,28},{24,16},{28,20},{32,40},... | collective-permute-start | bytes 393224 | tf_op jit(solution)/shard_map/ppermute | solution.py:283
  94.9 4.8 %collective-permute-done.9.y1 = f32[32,1024]{1,0:T(8,128)S(1)} collective-permute-done((f32[32,1024]{1,0:T(8,128)}, f32[32,1024]{1,0:T(8,128)S(1)}, u32[]{:S(2)}, u32[]{:S(2)}) %collective-permute-start.9) | collective-permute-done | bytes 131104 | tf_op jit(solution)/shard_map/ppermute | solution.py:283
  99.7 0.0 copy-start.11
  99.7 0.0 collective-permute-done.7.y2
  99.7 0.0 copy-start.4
  99.7 4.2 %collective-permute-done.8.y3 = f32[64,1024]{1,0:T(8,128)S(1)} collective-permute-done((f32[64,1024]{1,0:T(8,128)}, f32[64,1024]{1,0:T(8,128)S(1)}, u32[]{:S(2)}, u32[]{:S(2)}) %collective-permute-start.8) | collective-permute-done | bytes 262176 | tf_op jit(solution)/shard_map/ppermute | solution.py:283
  103.9 0.0 copy-start.5
  103.9 0.0 copy-done.11
  103.9 0.0 copy-done.4
  103.9 0.7 copy-done.5
  104.6 1.9 %unroute.1 = f32[4,16,1024]{2,1,0:T(8,128)} custom-call(s32[1]{0:T(128)} %bitcast.zpos, f32[32,1024]{1,0:T(8,128)} %get-tuple-element.44.c0, f32[32,1024]{1,0:T(8,128)} %copy-done.11, f32[64,1024]{1,0:T(8,128)} %copy-done.4, f32[64,1024]{1,0:T(8,128)} %copy-done.5), custom_call_target="tpu_custom_call" | custom-call | tf_op jit(solution)/shard_map/unroute/pallas_call | solution.py:38
  106.5 3.4 %all-to-all-start.2 = ((f32[4,16,1024]{2,1,0:T(8,128)}), f32[4,16,1024]{2,1,0:T(8,128)S(1)}, u32[]{:S(2)}, u32[]{:S(2)}) async-start(f32[4,16,1024]{2,1,0:T(8,128)} %unroute.1), calls=%async_computation.2 | async-start | bytes 524288 | tf_op jit(solution)/shard_map/all_to_all | solution.py:286
  109.9 0.0 copy-done.12
  109.9 2.3 %collective-permute-start.6 = (f32[64,1024]{1,0:T(8,128)S(1)}, f32[64,1024]{1,0:T(8,128)S(1)}, u32[]{:S(2)}, u32[]{:S(2)}) collective-permute-start(f32[64,1024]{1,0:T(8,128)S(1)} %copy-done.12), channel_id=1, source_target_pairs={{0,8},{4,12},{8,0},{12,4},{16,24},{20,28},{24,16},{28,20},{32,40},... | collective-permute-start | bytes 786440 | tf_op jit(solution)/shard_map/ppermute | solution.py:283
  112.2 6.8 %collective-permute-done.6.y1a = f32[64,1024]{1,0:T(8,128)S(1)} collective-permute-done((f32[64,1024]{1,0:T(8,128)S(1)}, f32[64,1024]{1,0:T(8,128)S(1)}, u32[]{:S(2)}, u32[]{:S(2)}) %collective-permute-start.6) | collective-permute-done | bytes 262176 | tf_op jit(solution)/shard_map/ppermute | solution.py:283
  119.1 0.0 copy-start.9
  119.1 0.0 all-to-all-done.2.z_in
  119.1 0.0 copy-start.3
  119.1 0.7 copy-done.9
  119.8 0.1 copy-done.3
  119.9 3.2 %finish.1 = (f32[256,512]{1,0:T(8,128)}, f32[256,512]{1,0:T(8,128)}) custom-call(s32[1]{0:T(128)} %bitcast.zpos, f32[256,512]{1,0:T(8,128)} %get-tuple-element.37.dk0, f32[256,512]{1,0:T(8,128)} %get-tuple-element.38.dv0, f32[384,1024]{1,0:T(8,128)} %copy-done, f32[64,1024]{1,0:T(8,128)} %copy-done.9, f32[64,1024]{1,0:T(8,128)} %copy-done.4, ...), custom_call_target="tpu_custom_call" | custom-call | tf_op jit(solution)/shard_map/finish/pallas_call | solution.py:38
Async XLA Ops:
  3.1 12.1 %all-to-all-start = ((f32[4,16,1024]{2,1,0:T(8,128)}), f32[4,16,1024]{2,1,0:T(8,128)S(1)}, u32[]{:S(2)}, u32[]{:S(2)}) async-start(f32[4,16,1024]{2,1,0:T(8,128)} %get-tuple-element.28), calls=%async_computation | async-start | bytes 524288 | tf_op jit(solution)/shard_map/all_to_all | solution.py:286
  9.5 19.1 %collective-permute-start = (f32[64,1024]{1,0:T(8,128)}, f32[64,1024]{1,0:T(8,128)S(1)}, u32[]{:S(2)}, u32[]{:S(2)}) collective-permute-start(f32[64,1024]{1,0:T(8,128)} %get-tuple-element.27), channel_id=1, source_target_pairs={{0,8},{4,12},{8,0},{12,4},{16,24},{20,28},{24,16},{28,20},{32,40},... | collective-permute-start | bytes 786440 | tf_op jit(solution)/shard_map/ppermute | solution.py:283
  15.2 0.7 copy-start.2
  17.6 15.9 %collective-permute-start.3 = (f32[64,1024]{1,0:T(8,128)}, f32[64,1024]{1,0:T(8,128)S(1)}, u32[]{:S(2)}, u32[]{:S(2)}) collective-permute-start(f32[64,1024]{1,0:T(8,128)} %get-tuple-element.31), channel_id=1, source_target_pairs={{0,24},{4,28},{8,16},{12,20},{16,8},{20,12},{24,0},{28,4},{32,56},... | collective-permute-start | bytes 786440 | tf_op jit(solution)/shard_map/ppermute | solution.py:283
  24.2 9.4 %collective-permute-start.2 = (f32[64,1024]{1,0:T(8,128)}, f32[64,1024]{1,0:T(8,128)S(1)}, u32[]{:S(2)}, u32[]{:S(2)}) collective-permute-start(f32[64,1024]{1,0:T(8,128)} %get-tuple-element.31), channel_id=1, source_target_pairs={{0,16},{4,20},{8,24},{12,28},{16,0},{20,4},{24,8},{28,12},{32,48},... | collective-permute-start | bytes 786440 | tf_op jit(solution)/shard_map/ppermute | solution.py:283
  26.5 7.1 %collective-permute-start.1 = (f32[32,1024]{1,0:T(8,128)}, f32[32,1024]{1,0:T(8,128)S(1)}, u32[]{:S(2)}, u32[]{:S(2)}) collective-permute-start(f32[32,1024]{1,0:T(8,128)} %get-tuple-element.30.refs_5_), channel_id=1, source_target_pairs={{0,8},{4,12},{8,0},{12,4},{16,24},{20,28},{24,16},{28,20},{32,40},... | collective-permute-start | bytes 393224 | tf_op jit(solution)/shard_map/ppermute | solution.py:283
  28.6 5.0 %copy-start.6 = (f32[64,1024]{1,0:T(8,128)}, f32[64,1024]{1,0:T(8,128)S(1)}, u32[]{:S(2)}) copy-start(f32[64,1024]{1,0:T(8,128)S(1)} %collective-permute-done.refs_1_) | copy-start | bytes 786436
  33.6 0.7 copy-start.10
  33.6 0.7 copy-start.7
  33.6 0.8 copy-start.8
  37.0 9.4 %collective-permute-start.4 = (f32[384,1024]{1,0:T(8,128)}, f32[384,1024]{1,0:T(8,128)S(1)}, u32[]{:S(2)}, u32[]{:S(2)}) collective-permute-start(f32[384,1024]{1,0:T(8,128)} %pack.1.own), channel_id=1, source_target_pairs={{0,4},{4,0},{8,12},{12,8},{16,20},{20,16},{24,28},{28,24},{32,36},... | collective-permute-start | bytes 4718600 | tf_op jit(solution)/shard_map/ppermute | solution.py:283
  46.4 1.2 copy-start.1
  75.5 7.0 %collective-permute-start.5 = (f32[384,1024]{1,0:T(8,128)}, f32[384,1024]{1,0:T(8,128)S(1)}, u32[]{:S(2)}, u32[]{:S(2)}) collective-permute-start(f32[384,1024]{1,0:T(8,128)} %get-tuple-element.39), channel_id=1, source_target_pairs={{0,4},{4,0},{8,12},{12,8},{16,20},{20,16},{24,28},{28,24},{32,36},... | collective-permute-start | bytes 4718600 | tf_op jit(solution)/shard_map/ppermute | solution.py:283
  82.4 1.2 copy-start
  86.3 23.6 %copy-start.12 = (f32[64,1024]{1,0:T(8,128)S(1)}, f32[64,1024]{1,0:T(8,128)}, u32[]{:S(2)}) copy-start(f32[64,1024]{1,0:T(8,128)} %get-tuple-element.41) | copy-start | bytes 786436
  86.3 13.4 %collective-permute-start.7 = (f32[64,1024]{1,0:T(8,128)}, f32[64,1024]{1,0:T(8,128)S(1)}, u32[]{:S(2)}, u32[]{:S(2)}) collective-permute-start(f32[64,1024]{1,0:T(8,128)} %get-tuple-element.42), channel_id=1, source_target_pairs={{0,16},{4,20},{8,24},{12,28},{16,0},{20,4},{24,8},{28,12},{32,48},... | collective-permute-start | bytes 786440 | tf_op jit(solution)/shard_map/ppermute | solution.py:283
  90.4 13.5 %collective-permute-start.8 = (f32[64,1024]{1,0:T(8,128)}, f32[64,1024]{1,0:T(8,128)S(1)}, u32[]{:S(2)}, u32[]{:S(2)}) collective-permute-start(f32[64,1024]{1,0:T(8,128)} %get-tuple-element.43), channel_id=1, source_target_pairs={{0,24},{4,28},{8,16},{12,20},{16,8},{20,12},{24,0},{28,4},{32,56},... | collective-permute-start | bytes 786440 | tf_op jit(solution)/shard_map/ppermute | solution.py:283
  93.0 6.7 %collective-permute-start.9 = (f32[32,1024]{1,0:T(8,128)}, f32[32,1024]{1,0:T(8,128)S(1)}, u32[]{:S(2)}, u32[]{:S(2)}) collective-permute-start(f32[32,1024]{1,0:T(8,128)} %get-tuple-element.45), channel_id=1, source_target_pairs={{0,8},{4,12},{8,0},{12,4},{16,24},{20,28},{24,16},{28,20},{32,40},... | collective-permute-start | bytes 393224 | tf_op jit(solution)/shard_map/ppermute | solution.py:283
  99.7 4.2 %copy-start.11 = (f32[32,1024]{1,0:T(8,128)}, f32[32,1024]{1,0:T(8,128)S(1)}, u32[]{:S(2)}) copy-start(f32[32,1024]{1,0:T(8,128)S(1)} %collective-permute-done.9.y1) | copy-start | bytes 393220
  99.7 4.2 %copy-start.4 = (f32[64,1024]{1,0:T(8,128)}, f32[64,1024]{1,0:T(8,128)S(1)}, u32[]{:S(2)}) copy-start(f32[64,1024]{1,0:T(8,128)S(1)} %collective-permute-done.7.y2) | copy-start | bytes 786436
  103.9 0.7 copy-start.5
  106.5 12.6 %all-to-all-start.2 = ((f32[4,16,1024]{2,1,0:T(8,128)}), f32[4,16,1024]{2,1,0:T(8,128)S(1)}, u32[]{:S(2)}, u32[]{:S(2)}) async-start(f32[4,16,1024]{2,1,0:T(8,128)} %unroute.1), calls=%async_computation.2 | async-start | bytes 524288 | tf_op jit(solution)/shard_map/all_to_all | solution.py:286
  109.9 9.1 %collective-permute-start.6 = (f32[64,1024]{1,0:T(8,128)S(1)}, f32[64,1024]{1,0:T(8,128)S(1)}, u32[]{:S(2)}, u32[]{:S(2)}) collective-permute-start(f32[64,1024]{1,0:T(8,128)S(1)} %copy-done.12), channel_id=1, source_target_pairs={{0,8},{4,12},{8,0},{12,4},{16,24},{20,28},{24,16},{28,20},{32,40},... | collective-permute-start | bytes 786440 | tf_op jit(solution)/shard_map/ppermute | solution.py:283
  119.1 0.7 copy-start.9
  119.1 0.8 copy-start.3
where the time goes:
time: 124 us; the launch traced here: 123 us
  starting transfers between devices  44.8 us (36%)
  Pallas kernels  34 us (27%)
  waiting for transfers between devices  29.6 us (24%)
  blocking collectives  8.42 us (7%)
  local copies, waits for them, and re-layouts  5.41 us (4%)
    ppermute x10, starting transfers between devices, swap(): return lax.ppermute(x, 'seq', [(i, i ^ mask) for i in range(seq)])  35 us
    pallas_call x8, Pallas kernels, call(): pl.pallas_call(body, out_shape=out, in_specs=[SM] * scalars + [VM] * (len...  34 us
    ppermute x10, waiting for transfers between devices, swap(): return lax.ppermute(x, 'seq', [(i, i ^ mask) for i in range(seq)])  27.2 us
    all_to_all x2, starting transfers between devices, z_swap(): lax.all_to_all(x, 'seq', 0, 0, axis_index_groups=z_groups, tiled=True)  9.84 us
    all_to_all x1, blocking collectives, body(): got = lax.all_to_all(send, 'head', 0, 0, tiled=True)  8.42 us
    unnamed x26, local copies, waits for them, and re-layouts  5.41 us
  transfers between devices with their start and end apart: 12, of which 7 were waited for; matrix products, arithmetic and copies ran while one was open for 0% of the time, Pallas kernels for 1%

commit v1 on v0

v1 whole, which is shorter than its diff:
```python
import math

import jax
import jax.numpy as jnp
from jax import lax
from jax.experimental import pallas as pl
from jax.experimental.pallas import tpu as pltpu
from jax.sharding import PartitionSpec as P


D = 2048
HEADS = 16
EPS = 1e-05
HD = D // HEADS
INV_ROOT = 1.0 / math.sqrt(HD)
LOG2E = 1.0 / math.log(2.0)

L45 = ((16, 4), (16, 5))
GATHERED = ((64, 2),) + L45 + ((32, 3),) + L45 + ((32, 3),) + L45 + L45
LEVELS = ((256, 0), (128, 1)) + GATHERED + GATHERED
NEAR = 256
KEYS = sum(rows for rows, _ in LEVELS)

VM = pl.BlockSpec(memory_space=pltpu.VMEM)
HB = pl.BlockSpec(memory_space=pltpu.HBM)
F32 = jnp.float32
BF16 = jnp.bfloat16


def shape(*dims):
    return jax.ShapeDtypeStruct(dims, F32)


def call(body, out, args, spaces="", scratch=(), grant=16):
    spaces = spaces.ljust(len(args))
    kinds = {"s": pltpu.SMEM, "h": pltpu.HBM, " ": pltpu.VMEM}
    args = [pltpu.with_memory_space_constraint(x, pltpu.HBM) if c == "h" else x for x, c in zip(args, spaces)]
    return pl.pallas_call(
        body,
        out_shape=out,
        in_specs=[pl.BlockSpec(memory_space=kinds[c]) for c in spaces],
        out_specs=jax.tree.map(lambda x: HB if isinstance(x, pl.MemoryRef) else VM, out),
        scratch_shapes=scratch,
        compiler_params=pltpu.CompilerParams(vmem_limit_bytes=grant << 20),
    )(*args)


def staging(count):
    return [pltpu.VMEM((count, 4, NEAR, HD), F32), pltpu.SemaphoreType.DMA((count, 4))]


class Staged:
    def __init__(self, refs, buf, sem):
        self.buf, self.copies = buf, {}
        for h in range(4):
            for i, ref in enumerate(refs):
                copy = pltpu.make_async_copy(ref.at[:, pl.ds(h * HD, HD)], buf.at[i, h], sem.at[i, h])
                copy.start()
                self.copies[i, h] = copy

    def wait(self, i, h):
        if (i, h) in self.copies:
            self.copies.pop((i, h)).wait()

    def at(self, i, h):
        self.wait(i, h)
        return self.buf[i, h]


def halves(value, buf):
    rows = value.shape[0] // 2
    buf[...] = value
    return 0.5 * (buf[pl.ds(0, rows, stride=2), :] + buf[pl.ds(1, rows, stride=2), :])


def doubled(value, buf):
    rows = value.shape[0]
    half = 0.5 * value
    buf[pl.ds(0, rows, stride=2), :] = half
    buf[pl.ds(1, rows, stride=2), :] = half
    return buf[...]


def buffers(count, *rows):
    return [pltpu.VMEM((count, n, HD), F32) for n in rows]


def coarsen_body(k_hbm, v_hbm, l1, l2, l3, l4, kv, sem, b1, b2, b3):
    staged = Staged((k_hbm, v_hbm), kv, sem)
    for h in range(8):
        i, j = h // 4, h % 4
        staged.wait(i, j)
        to = slice(h * HD, (h + 1) * HD)
        one = 0.5 * (kv[i, j, pl.ds(0, 128, stride=2), :] + kv[i, j, pl.ds(1, 128, stride=2), :])
        l1[:, to] = one
        two = halves(one, b1.at[h])
        l2[:, to] = two
        three = halves(two, b2.at[h])
        l3[:, to] = three
        four = halves(three, b3.at[h])
        for j in range(4):
            l4[j, :, to] = four


def route_body(zpos, z_in, l3, c0, y23, buf):
    z = zpos[0]
    c0[0:16, :] = z_in[z ^ 1]
    for h in range(8):
        to = slice(h * HD, (h + 1) * HD)
        for j in (2, 3):
            c0[8 * j : 8 * j + 8, to] = halves(z_in[z ^ j, :, to], buf.at[2 * h + j - 2])
    y23[0:32, :] = l3[...]
    y23[32:64, :] = c0[...]


def pack_body(*refs):
    out = refs[-1]
    row = 0
    for ref in refs[:-1]:
        out[row : row + ref.shape[0], :] = ref[...]
        row += ref.shape[0]


def split2(x):
    hi = x.astype(BF16)
    return hi, (x - hi.astype(F32)).astype(BF16)


def split3(x):
    hi = x.astype(BF16)
    rest = x - hi.astype(F32)
    mid = rest.astype(BF16)
    return hi, mid, (rest - mid.astype(F32)).astype(BF16)


NT = (((1,), (1,)), ((), ()))
NN = (((1,), (0,)), ((), ()))
TN = (((0,), (0,)), ((), ()))


def dot(a, b, dims):
    return lax.dot_general(a, b, dims, preferred_element_type=F32)


def cat(*parts):
    return jnp.concatenate(parts, axis=1)


def scores(keys, query):
    kh, km, kl = split3(keys)
    qh, qm, ql = split3(query)
    key2 = cat(kh, km)
    return dot(key2, cat(qh, qh), NT) + (dot(key2, cat(qm, qm), NT) + dot(cat(kh, kl), cat(ql, qh), NT))


def dot_nt(a, b):
    ah, al = split2(a)
    bh, bl = split2(b)
    return dot(cat(ah, al), cat(bh, bh), NT) + dot(ah, bl, NT)


def dot_nn(ah, al, b):
    bh, bl = split2(b)
    both = dot(ah, cat(bh, bl), NN)
    half = b.shape[1]
    return both[:, :half] + both[:, half:] + dot(al, bh, NN)


def dot_tn(a, bh, bl):
    ah, al = split2(a)
    return dot(ah, bh, TN) + (dot(ah, bl, TN) + dot(al, bh, TN))


def head_cols(h):
    return slice(h * HD, (h + 1) * HD)


def gather(near, refs, at):
    return jnp.concatenate([near] + [ref[:, at] for ref in refs], axis=0)


def near_body(q_hbm, k_hbm, v_hbm, ct_hbm, q, k, v, ct, s_out, sem):
    copies = []
    for i, (src, dst) in enumerate(((q_hbm, q), (k_hbm, k), (v_hbm, v), (ct_hbm, ct))):
        copies.append(pltpu.make_async_copy(src, dst, sem.at[i]))
        copies[i].start()
    copies[0].wait()
    copies[1].wait()
    for h in range(4):
        at = head_cols(h)
        s_out[h] = scores(k[:, at], q[:, at] * (INV_ROOT * LOG2E))
    copies[2].wait()
    copies[3].wait()


def forward_body(q_ref, k_ref, v_ref, ct, one, own, peer, gain, s_near, p_out, att, send):
    far = (one, own, peer)
    for h in range(4):
        at = head_cols(h)
        query = q_ref[:, at] * (INV_ROOT * LOG2E)
        vat = head_cols(4 + h)
        blocks = [s_near[h]] + [scores(ref[:, at], query) for ref in far]
        s = jnp.concatenate(blocks, axis=0)
        parts = []
        row = 0
        for rows, level in LEVELS:
            seg = s[row : row + rows]
            parts.append(seg + float(level) if level else seg)
            row += rows
        s = jnp.concatenate(parts, axis=0)
        top = jnp.max(s, axis=0, keepdims=True)
        e = jnp.exp2(s - top)
        p = e * (1.0 / jnp.sum(e, axis=0, keepdims=True))
        p_out[h] = p
        values = gather(v_ref[:, at], far, vat)
        ph, pl_ = split2(p)
        att[:, at] = dot_tn(values, ph, pl_).T
    a = att[...]
    width = 4 * HD
    total = jnp.sum(a, axis=1, keepdims=True)
    mean = total * (1.0 / width)
    away = a - mean
    sg = ct[...] * gain[...]
    lane = lax.broadcasted_iota(jnp.int32, (NEAR, HD), 1)
    stats = jnp.where(lane == 0, mean, 0.0)
    for j, value in (
        (1, jnp.sum(away * away, axis=1, keepdims=True)),
        (2, jnp.sum(sg, axis=1, keepdims=True)),
        (3, jnp.sum(sg * away, axis=1, keepdims=True)),
    ):
        stats = jnp.where(lane == j, value, stats)
    rows = stats.T[0:8]
    for j in range(4):
        send[j] = rows


def backward_body(
    q_ref, k_ref, v_ref, ct, one, own, peer, gain, bias, p_in, att, got,
    normed, dq, dv, d_one, dk, d_own, d_peer, out_buf, out_sem,
):
    written = []

    def write(i, h, ref, value, col=None):
        rows = value.shape[0]
        out_buf[i, h, 0:rows, :] = value
        to = ref.at[:, pl.ds((h if col is None else col) * HD, HD)]
        copy = pltpu.make_async_copy(out_buf.at[i, h, pl.ds(0, rows)], to, out_sem.at[i, h])
        copy.start()
        written.append(copy)

    far = (one, own, peer)
    stat = [got[j] for j in range(4)]
    mean = (stat[0][0:1] + stat[1][0:1] + stat[2][0:1] + stat[3][0:1]) * 0.25
    square = jnp.zeros_like(mean)
    total = jnp.zeros_like(mean)
    cross = jnp.zeros_like(mean)
    for part in stat:
        shift = part[0:1] - mean
        square = square + (part[1:2] + (4.0 * HD) * (shift * shift))
        total = total + part[2:3]
        cross = cross + (part[3:4] + part[2:3] * shift)
    inv = lax.rsqrt(square * (1.0 / D) + EPS)
    cross = cross * inv
    sub = lax.broadcasted_iota(jnp.int32, (HD, NEAR), 0)
    table = jnp.where(sub == 0, mean, 0.0)
    for j, value in ((1, inv), (2, total * (1.0 / D)), (3, cross * (1.0 / D))):
        table = jnp.where(sub == j, value, table)
    cols = table.T
    mean, inv, total, cross = (cols[:, j : j + 1] for j in range(4))
    for h in range(4):
        at = head_cols(h)
        vat = head_cols(4 + h)
        hat = (att[:, at] - mean) * inv
        write(0, h, normed, hat * gain[:, at] + bias[:, at])
        g = inv * (ct[:, at] * gain[:, at] - total - hat * cross)
        p = p_in[h]
        values = gather(v_ref[:, at], far, vat)
        keys = gather(k_ref[:, at], far, at)
        dp = dot_nt(values, g * INV_ROOT)
        ph, pl_ = split2(p)
        dval = dot_nn(ph, pl_, g)
        write(2, h, dv, dval[0:256])
        ds = p * (dp - jnp.sum(p * dp, axis=0, keepdims=True))
        sh, sl = split2(ds)
        dkey = dot_nn(sh, sl, q_ref[:, at])
        write(1, h, dq, dot_tn(keys, sh, sl).T)
        dk[:, at] = dkey[0:256]
        write(3, h, d_one, dkey[256:384])
        write(4, h, d_one, dval[256:384], 4 + h)
        row = NEAR + 128
        for ref in (d_own, d_peer):
            n = ref.shape[0]
            ref[:, at] = dkey[row : row + n]
            ref[:, vat] = dval[row : row + n]
            row += n
    for copy in written:
        copy.wait()


def sum_body(ypos, mine, got, g1, g2, g3, gb):
    y = ypos[0]

    def both(row, n):
        return mine[row : row + n, :] + got[row : row + n, :]

    g1[...] = both(0, 64)
    gb[y ^ 1] = both(64, 32)
    g2[...] = both(96, 32)
    gb[y ^ 2] = both(128, 32)
    g3[...] = both(160, 32)
    gb[y ^ 3] = both(192, 32)
    gb[y] = both(224, 32)


def unroute_body(zpos, y_in, send, buf):
    z = zpos[0]
    g = (y_in[0] + y_in[1]) + (y_in[2] + y_in[3])
    send[z] = jnp.zeros((16, 8 * HD), F32)
    send[z ^ 1] = g[0:16]
    for j in (2, 3):
        for h in range(8):
            to = slice(h * HD, (h + 1) * HD)
            send[z ^ j, :, to] = doubled(g[8 * j : 8 * j + 8, to], buf.at[2 * h + j - 2])


def finish_body(zpos, dk0, dv0, got, y1a, y2, y3, z_in, dk, dv, near, sem, s3, s2, s1, s0):
    staged = Staged((dv0,), near, sem)
    z = zpos[0]
    for h in range(8):
        to = slice(h * HD, (h + 1) * HD)
        part = z_in[z ^ 1, :, to] + (z_in[z ^ 2, :, to] + z_in[z ^ 3, :, to])
        part = doubled(part, s3.at[h]) + (y2[:, to] + y3[:, to])
        part = doubled(part, s2.at[h]) + y1a[:, to]
        part = doubled(part, s1.at[h]) + got[:, to]
        at = head_cols(h % 4)
        part = doubled(part, s0.at[h])
        if h < 4:
            dk[:, at] = dk0[:, at] + part
        else:
            dv[:, at] = staged.at(0, h % 4) + part


def body(query, key, value, cotangent, gain, bias):
    seq = lax.axis_size("seq")
    zpos = (lax.axis_index("seq") // 8 % 4).reshape(1).astype(jnp.int32)
    ypos = (lax.axis_index("seq") // 2 % 4).reshape(1).astype(jnp.int32)
    z_groups = [[zh * 32 + zl * 8 + r for zl in range(4)] for zh in range(seq // 32) for r in range(8)]
    y_groups = [[z * 8 + y * 2 + c for y in range(4)] for z in range(seq // 8) for c in range(2)]

    def swap(x, mask):
        return lax.ppermute(x, "seq", [(i, i ^ mask) for i in range(seq)])

    def exchange(x, groups):
        return lax.all_to_all(x, "seq", 0, 0, axis_index_groups=groups, tiled=True)

    gain = gain.reshape(1, -1)
    bias = bias.reshape(1, -1)
    l1, l2, l3, l4 = call(
        coarsen_body,
        (shape(128, 1024), shape(64, 1024), shape(32, 1024), shape(4, 16, 1024)),
        (key, value),
        "hh",
        staging(2) + buffers(8, 128, 64, 32),
    )
    z_in = exchange(l4, z_groups)
    y1 = swap(l2, 2)
    one = swap(l1, 1)
    c0, y23 = call(
        route_body, (shape(32, 1024), shape(64, 1024)), (zpos, z_in, l3), "s", buffers(16, 16)
    )
    y2 = swap(y23, 4)
    y3 = swap(y23, 6)
    c1 = swap(c0, 2)
    own = call(pack_body, shape(256, 1024), (y1, c1, y2, y3, c0))
    peer = swap(own, 1)
    q, k, v, ct, s_near = call(
        near_body,
        (shape(256, 512),) * 4 + (shape(4, NEAR, NEAR),),
        (query, key, value, cotangent),
        "hhhh",
        [pltpu.SemaphoreType.DMA((4,))],
    )
    inputs = (q, k, v, ct, one, own, peer, gain)
    p, att, send = call(
        forward_body, (shape(4, KEYS, NEAR), shape(256, 512), shape(4, 8, 256)), inputs + (s_near,)
    )
    got = lax.all_to_all(send, "head", 0, 0, tiled=True)
    normed, dq, dv0, d_one, dk0, d_own, d_peer = call(
        backward_body,
        (pltpu.HBM((256, 512), F32),) * 3
        + (pltpu.HBM((128, 1024), F32), shape(256, 512), shape(256, 1024), shape(256, 1024)),
        inputs + (bias, p, att, got),
        scratch=staging(5),
    )
    d_got = swap(d_peer, 1)
    g1, g2, g3, gb = call(
        sum_body,
        (shape(64, 1024), shape(32, 1024), shape(32, 1024), shape(4, 32, 1024)),
        (ypos, d_own, d_got),
        "s",
    )
    y_got = exchange(gb, y_groups)
    r1 = swap(g1, 2)
    r2 = swap(g2, 4)
    r3 = swap(g3, 6)
    z_send = call(unroute_body, shape(4, 16, 1024), (zpos, y_got), "s", buffers(16, 16))
    z_got = exchange(z_send, z_groups)
    got_one = swap(d_one, 1)
    dk, dv = call(
        finish_body,
        (shape(256, 512), shape(256, 512)),
        (zpos, dk0, dv0, got_one, r1, r2, r3, z_got),
        "s h",
        staging(1) + buffers(8, 32, 64, 128, 256),
    )
    return normed, dq, dk, dv


def solution(mesh):
    both = P("seq", "head")
    return jax.shard_map(
        body,
        mesh=mesh,
        in_specs=(both,) * 4 + (P("head"),) * 2,
        out_specs=(both,) * 4,
        check_vma=False,
    )
```

time: 124 us -> 107 us (0.86)
  Pallas kernels: 34 us -> 19.9 us
  waiting for transfers between devices: 29.6 us -> 16.3 us
  blocking collectives: 8.42 us -> 19.8 us
  local copies, waits for them, and re-layouts: 5.41 us -> 0.01 us
  starting transfers between devices: 44.8 us -> 49.6 us
    pallas_call x8 -> x9, Pallas kernels: 34 us -> 19.9 us  [call(): pl.pallas_call(body, out_shape=out, in_specs=[pl.BlockSpec(memory_space=k...]
    ppermute x10 -> x11, waiting for transfers between devices: 27.2 us -> 13.9 us  [swap(): return lax.ppermute(x, 'seq', [(i, i ^ mask) for i in range(seq)])]
    all_to_all x0 -> x1, blocking collectives: none -> 11.7 us  [exchange(): return lax.all_to_all(x, 'seq', 0, 0, axis_index_groups=groups, tiled=True)]
    unnamed x26 -> x4, local copies, waits for them, and re-layouts: 5.41 us -> 0.01 us
    ppermute x10 -> x11, starting transfers between devices: 35 us -> 39.7 us  [swap(): return lax.ppermute(x, 'seq', [(i, i ^ mask) for i in range(seq)])]
  transfers between devices with their start and end apart: 12 -> 13, of which waited for: 7 -> 5; matrix products, arithmetic and copies ran while one was open for 0% -> 0% of each run, Pallas kernels for 1% -> 2%
where the time goes in v1:
time: 107 us; the launch traced here: 106 us
  starting transfers between devices  49.6 us (46%)
  Pallas kernels  19.9 us (19%)
  blocking collectives  19.8 us (19%)
  waiting for transfers between devices  16.3 us (15%)
    ppermute x11, starting transfers between devices, swap(): return lax.ppermute(x, 'seq', [(i, i ^ mask) for i in range(seq)])  39.7 us
    pallas_call x9, Pallas kernels, call(): pl.pallas_call(body, out_shape=out, in_specs=[pl.BlockSpec(memory_space=k...  19.9 us
    ppermute x11, waiting for transfers between devices, swap(): return lax.ppermute(x, 'seq', [(i, i ^ mask) for i in range(seq)])  13.9 us
    all_to_all x1, blocking collectives, exchange(): return lax.all_to_all(x, 'seq', 0, 0, axis_index_groups=groups, tiled=True)  11.7 us
    all_to_all x2, starting transfers between devices, exchange(): return lax.all_to_all(x, 'seq', 0, 0, axis_index_groups=groups, tiled=True)  9.85 us
    all_to_all x1, blocking collectives, body(): got = lax.all_to_all(send, 'head', 0, 0, tiled=True)  8.11 us
    all_to_all x2, waiting for transfers between devices, exchange(): return lax.all_to_all(x, 'seq', 0, 0, axis_index_groups=groups, tiled=True)  2.4 us
  transfers between devices with their start and end apart: 13, of which 5 were waited for; matrix products, arithmetic and copies ran while one was open for 0% of the time, Pallas kernels for 2%

profile of v1, /device:TPU:1, one launch (start us, length us, event | category | flops | bytes accessed | tf_op | source)
XLA Modules:
  0.0 106.4 jit_solution(3576444318658839025)
XLA Ops:
  0.6 0.0 copy-start
  0.6 2.3 %shard_map.94 = (f32[128,1024]{1,0:T(8,128)S(1)}, f32[64,1024]{1,0:T(8,128)S(1)}, f32[32,1024]{1,0:T(8,128)S(1)}, f32[4,16,1024]{2,1,0:T(8,128)}) custom-call(f32[256,512]{1,0:T(8,128)} %k_hbm.3, f32[256,512]{1,0:T(8,128)} %v_hbm.3), custom_call_target="tpu_custom_call" | custom-call | tf_op jit(solution)/shard_map/pallas_call | solution.py:38
  2.9 6.4 %all-to-all-start = ((f32[4,16,1024]{2,1,0:T(8,128)}), f32[4,16,1024]{2,1,0:T(8,128)S(1)}, u32[]{:S(2)}, u32[]{:S(2)}) async-start(f32[4,16,1024]{2,1,0:T(8,128)} %get-tuple-element.37), calls=%async_computation | async-start | bytes 524288 | tf_op jit(solution)/shard_map/all_to_all | solution.py:354
  9.4 3.2 %collective-permute-start.1 = (f32[64,1024]{1,0:T(8,128)S(1)}, f32[64,1024]{1,0:T(8,128)S(1)}, u32[]{:S(2)}, u32[]{:S(2)}) collective-permute-start(f32[64,1024]{1,0:T(8,128)S(1)} %get-tuple-element.36), channel_id=1, source_target_pairs={{0,8},{4,12},{8,0},{12,4},{16,24},{20,28},{24,16},{28,20},{32,40},... | collective-permute-start | bytes 786440 | tf_op jit(solution)/shard_map/ppermute | solution.py:351
  12.6 2.4 %all-to-all-done.z_in = f32[4,16,1024]{2,1,0:T(8,128)S(1)} async-done(((f32[4,16,1024]{2,1,0:T(8,128)}), f32[4,16,1024]{2,1,0:T(8,128)S(1)}, u32[]{:S(2)}, u32[]{:S(2)}) %all-to-all-start) | async-done | bytes 262176 | tf_op jit(solution)/shard_map/all_to_all | solution.py:354
  15.0 6.6 %collective-permute-start.4 = (f32[64,1024]{1,0:T(8,128)S(1)}, f32[64,1024]{1,0:T(8,128)S(1)}, u32[]{:S(2)}, u32[]{:S(2)}) collective-permute-start(f32[64,1024]{1,0:T(8,128)S(1)} %get-tuple-element.40), channel_id=1, source_target_pairs={{0,24},{4,28},{8,16},{12,20},{16,8},{20,12},{24,0},{28,4},{32,56},... | collective-permute-start | bytes 786440 | tf_op jit(solution)/shard_map/ppermute | solution.py:351
  21.6 2.3 %collective-permute-start.3 = (f32[64,1024]{1,0:T(8,128)S(1)}, f32[64,1024]{1,0:T(8,128)S(1)}, u32[]{:S(2)}, u32[]{:S(2)}) collective-permute-start(f32[64,1024]{1,0:T(8,128)S(1)} %get-tuple-element.40), channel_id=1, source_target_pairs={{0,16},{4,20},{8,24},{12,28},{16,0},{20,4},{24,8},{28,12},{32,48},... | collective-permute-start | bytes 786440 | tf_op jit(solution)/shard_map/ppermute | solution.py:351
  23.9 2.1 %collective-permute-start.2 = (f32[32,1024]{1,0:T(8,128)S(1)}, f32[32,1024]{1,0:T(8,128)S(1)}, u32[]{:S(2)}, u32[]{:S(2)}) collective-permute-start(f32[32,1024]{1,0:T(8,128)S(1)} %get-tuple-element.39.refs_4_), channel_id=1, source_target_pairs={{0,8},{4,12},{8,0},{12,4},{16,24},{20,28},{24,16},{28,20},{32,40},... | collective-permute-start | bytes 393224 | tf_op jit(solution)/shard_map/ppermute | solution.py:351
  26.0 0.0 collective-permute-done.1.refs_0_
  26.0 4.7 %collective-permute-done.2.refs_1_ = f32[32,1024]{1,0:T(8,128)S(1)} collective-permute-done((f32[32,1024]{1,0:T(8,128)S(1)}, f32[32,1024]{1,0:T(8,128)S(1)}, u32[]{:S(2)}, u32[]{:S(2)}) %collective-permute-start.2) | collective-permute-done | bytes 131104 | tf_op jit(solution)/shard_map/ppermute | solution.py:351
  30.8 0.0 collective-permute-done.4.refs_3_
  30.8 0.0 collective-permute-done.3.refs_2_
  30.8 0.1 shard_map.96.own
  30.8 6.3 %collective-permute-start.5 = (f32[256,1024]{1,0:T(8,128)S(1)}, f32[256,1024]{1,0:T(8,128)S(1)}, u32[]{:S(2)}, u32[]{:S(2)}) collective-permute-start(f32[256,1024]{1,0:T(8,128)S(1)} %shard_map.96.own), channel_id=1, source_target_pairs={{0,4},{4,0},{8,12},{12,8},{16,20},{20,16},{24,28},{28,24},{32,36},... | collective-permute-start | bytes 3145736 | tf_op jit(solution)/shard_map/ppermute | solution.py:351
  37.2 0.0 copy-start.1
  37.2 1.9 %collective-permute-start = (f32[128,1024]{1,0:T(8,128)S(1)}, f32[128,1024]{1,0:T(8,128)S(1)}, u32[]{:S(2)}, u32[]{:S(2)}) collective-permute-start(f32[128,1024]{1,0:T(8,128)S(1)} %get-tuple-element.35), channel_id=1, source_target_pairs={{0,4},{4,0},{8,12},{12,8},{16,20},{20,16},{24,28},{28,24},{32,36},... | collective-permute-start | bytes 1572872 | tf_op jit(solution)/shard_map/ppermute | solution.py:351
  39.1 1.9 %shard_map.93 = (f32[256,512]{1,0:T(8,128)S(1)}, f32[256,512]{1,0:T(8,128)S(1)}, f32[256,512]{1,0:T(8,128)S(1)}, f32[256,512]{1,0:T(8,128)S(1)}, f32[4,256,256]{2,1,0:T(8,128)S(1)}) custom-call(f32[256,512]{1,0:T(8,128)} %q_hbm.1, f32[256,512]{1,0:T(8,128)} %k_hbm.3, f32[256,512]{1,0:T(8,128)} %v_hbm.3, f32[256,512]{1,0:T(8,128)} %ct_hbm.1), custom_call_target="tpu_custom_call" | custom-call | tf_op jit(solution)/shard_map/pallas_call | solution.py:38
  41.0 0.0 collective-permute-done.one
  41.0 0.0 collective-permute-done.5.peer
  41.0 0.0 copy-done
  41.0 5.2 %shard_map.97 = (f32[4,896,256]{2,1,0:T(8,128)S(1)}, f32[256,512]{1,0:T(8,128)S(1)}, f32[4,8,256]{2,1,0:T(8,128)S(1)}) custom-call(f32[256,512]{1,0:T(8,128)S(1)} %get-tuple-element.31.q_ref, f32[256,512]{1,0:T(8,128)S(1)} %get-tuple-element.32.k_ref, f32[256,512]{1,0:T(8,128)S(1)} %get-tuple-element.33.v_ref, f32[256,512]{1,0:T(8,128)S(1)} %get-tuple-element.34.ct, ...), custom_call_target="tpu_custom_call" | custom-call | tf_op jit(solution)/shard_map/pallas_call | solution.py:38
  46.2 8.1 %all_to_all.20.got = f32[4,8,256]{2,1,0:T(8,128)S(1)} all-to-all(f32[4,8,256]{2,1,0:T(8,128)S(1)} %get-tuple-element.44), channel_id=1, replica_groups=mesh['seq'=128,'head'=4] {'head'}, dimensions={0} | all-to-all | bytes 65536 | tf_op jit(solution)/shard_map/all_to_all | solution.py:387
  54.3 0.0 copy-done.1
  54.3 7.5 %shard_map.98 = (f32[256,512]{1,0:T(8,128)}, f32[256,512]{1,0:T(8,128)}, f32[256,512]{1,0:T(8,128)}, f32[128,1024]{1,0:T(8,128)}, f32[256,512]{1,0:T(8,128)S(1)}...) custom-call(f32[256,512]{1,0:T(8,128)S(1)} %get-tuple-element.31.q_ref, f32[256,512]{1,0:T(8,128)S(1)} %get-tuple-element.32.k_ref, ...), custom_call_target="tpu_custom_call" | custom-call | tf_op jit(solution)/shard_map/pallas_call | solution.py:38
  61.8 3.8 %collective-permute-start.7 = (f32[256,1024]{1,0:T(8,128)}, f32[256,1024]{1,0:T(8,128)S(1)}, u32[]{:S(2)}, u32[]{:S(2)}) collective-permute-start(f32[256,1024]{1,0:T(8,128)} %get-tuple-element.51), channel_id=1, source_target_pairs={{0,4},{4,0},{8,12},{12,8},{16,20},{20,16},{24,28},{28,24},{32,36},... | collective-permute-start | bytes 3145736 | tf_op jit(solution)/shard_map/ppermute | solution.py:351
  65.7 2.4 %collective-permute-done.7.got = f32[256,1024]{1,0:T(8,128)S(1)} collective-permute-done((f32[256,1024]{1,0:T(8,128)}, f32[256,1024]{1,0:T(8,128)S(1)}, u32[]{:S(2)}, u32[]{:S(2)}) %collective-permute-start.7) | collective-permute-done | bytes 1048608 | tf_op jit(solution)/shard_map/ppermute | solution.py:351
  68.2 0.1 shard_map.99
  68.3 11.7 %all_to_all.21.y_in = f32[4,32,1024]{2,1,0:T(8,128)S(1)} all-to-all(f32[4,32,1024]{2,1,0:T(8,128)S(1)} %get-tuple-element.55), channel_id=1, replica_groups={{0,8,16,24},{4,12,20,28},{32,40,48,56},{36,44,52,60},{64,72,80,88},{68,..., dimensions={0} | all-to-all | bytes 1048576 | tf_op jit(solution)/shard_map/all_to_all | solution.py:354
  79.9 0.8 shard_map.100
  80.7 3.4 %all-to-all-start.3 = ((f32[4,16,1024]{2,1,0:T(8,128)}), f32[4,16,1024]{2,1,0:T(8,128)S(1)}, u32[]{:S(2)}, u32[]{:S(2)}) async-start(f32[4,16,1024]{2,1,0:T(8,128)} %shard_map.100), calls=%async_computation.3 | async-start | bytes 524288 | tf_op jit(solution)/shard_map/all_to_all | solution.py:354
  84.1 3.9 %collective-permute-start.6 = (f32[128,1024]{1,0:T(8,128)}, f32[128,1024]{1,0:T(8,128)S(1)}, u32[]{:S(2)}, u32[]{:S(2)}) collective-permute-start(f32[128,1024]{1,0:T(8,128)} %get-tuple-element.49), channel_id=1, source_target_pairs={{0,4},{4,0},{8,12},{12,8},{16,20},{20,16},{24,28},{28,24},{32,36},... | collective-permute-start | bytes 1572872 | tf_op jit(solution)/shard_map/ppermute | solution.py:351
  88.0 2.2 %collective-permute-start.8 = (f32[64,1024]{1,0:T(8,128)S(1)}, f32[64,1024]{1,0:T(8,128)S(1)}, u32[]{:S(2)}, u32[]{:S(2)}) collective-permute-start(f32[64,1024]{1,0:T(8,128)S(1)} %get-tuple-element.52), channel_id=1, source_target_pairs={{0,8},{4,12},{8,0},{12,4},{16,24},{20,28},{24,16},{28,20},{32,40},... | collective-permute-start | bytes 786440 | tf_op jit(solution)/shard_map/ppermute | solution.py:351
  90.2 3.7 %collective-permute-start.9 = (f32[32,1024]{1,0:T(8,128)S(1)}, f32[32,1024]{1,0:T(8,128)S(1)}, u32[]{:S(2)}, u32[]{:S(2)}) collective-permute-start(f32[32,1024]{1,0:T(8,128)S(1)} %get-tuple-element.53), channel_id=1, source_target_pairs={{0,16},{4,20},{8,24},{12,28},{16,0},{20,4},{24,8},{28,12},{32,48},... | collective-permute-start | bytes 393224 | tf_op jit(solution)/shard_map/ppermute | solution.py:351
  93.9 3.7 %collective-permute-start.10 = (f32[32,1024]{1,0:T(8,128)S(1)}, f32[32,1024]{1,0:T(8,128)S(1)}, u32[]{:S(2)}, u32[]{:S(2)}) collective-permute-start(f32[32,1024]{1,0:T(8,128)S(1)} %get-tuple-element.54), channel_id=1, source_target_pairs={{0,24},{4,28},{8,16},{12,20},{16,8},{20,12},{24,0},{28,4},{32,56},... | collective-permute-start | bytes 393224 | tf_op jit(solution)/shard_map/ppermute | solution.py:351
  97.6 0.0 collective-permute-done.6.got
  97.6 3.5 %collective-permute-done.9.y2 = f32[32,1024]{1,0:T(8,128)S(1)} collective-permute-done((f32[32,1024]{1,0:T(8,128)S(1)}, f32[32,1024]{1,0:T(8,128)S(1)}, u32[]{:S(2)}, u32[]{:S(2)}) %collective-permute-start.9) | collective-permute-done | bytes 131104 | tf_op jit(solution)/shard_map/ppermute | solution.py:351
  101.1 3.2 %collective-permute-done.10.y3 = f32[32,1024]{1,0:T(8,128)S(1)} collective-permute-done((f32[32,1024]{1,0:T(8,128)S(1)}, f32[32,1024]{1,0:T(8,128)S(1)}, u32[]{:S(2)}, u32[]{:S(2)}) %collective-permute-start.10) | collective-permute-done | bytes 131104 | tf_op jit(solution)/shard_map/ppermute | solution.py:351
  104.3 0.0 collective-permute-done.8.y1a
  104.3 0.0 all-to-all-done.3.z_in
  104.3 2.1 %shard_map.101 = (f32[256,512]{1,0:T(8,128)}, f32[256,512]{1,0:T(8,128)}) custom-call(s32[1]{0:T(128)} %bitcast.zpos, f32[256,512]{1,0:T(8,128)S(1)} %get-tuple-element.47.dk0, f32[256,512]{1,0:T(8,128)} %get-tuple-element.48.dv0, f32[128,1024]{1,0:T(8,128)S(1)} %collective-permute-done.6.got, f32[64,1024]{1,0:T(8,128)S(1)} %collective-permute-done.8.y1a, ...), custom_call_target="tpu_custom_call" | custom-call | tf_op jit(solution)/shard_map/pallas_call | solution.py:38
  (1 shorter events, 0.0 us)
Async XLA Ops:
  0.6 40.4 %copy-start = (f32[512]{0:T(512)S(1)}, f32[512]{0:T(512)}, u32[]{:S(2)}) copy-start(f32[512]{0:T(512)} %param.10) | copy-start | bytes 6148
  2.9 12.1 %all-to-all-start = ((f32[4,16,1024]{2,1,0:T(8,128)}), f32[4,16,1024]{2,1,0:T(8,128)S(1)}, u32[]{:S(2)}, u32[]{:S(2)}) async-start(f32[4,16,1024]{2,1,0:T(8,128)} %get-tuple-element.37), calls=%async_computation | async-start | bytes 524288 | tf_op jit(solution)/shard_map/all_to_all | solution.py:354
  9.4 16.7 %collective-permute-start.1 = (f32[64,1024]{1,0:T(8,128)S(1)}, f32[64,1024]{1,0:T(8,128)S(1)}, u32[]{:S(2)}, u32[]{:S(2)}) collective-permute-start(f32[64,1024]{1,0:T(8,128)S(1)} %get-tuple-element.36), channel_id=1, source_target_pairs={{0,8},{4,12},{8,0},{12,4},{16,24},{20,28},{24,16},{28,20},{32,40},... | collective-permute-start | bytes 786440 | tf_op jit(solution)/shard_map/ppermute | solution.py:351
  15.0 15.7 %collective-permute-start.4 = (f32[64,1024]{1,0:T(8,128)S(1)}, f32[64,1024]{1,0:T(8,128)S(1)}, u32[]{:S(2)}, u32[]{:S(2)}) collective-permute-start(f32[64,1024]{1,0:T(8,128)S(1)} %get-tuple-element.40), channel_id=1, source_target_pairs={{0,24},{4,28},{8,16},{12,20},{16,8},{20,12},{24,0},{28,4},{32,56},... | collective-permute-start | bytes 786440 | tf_op jit(solution)/shard_map/ppermute | solution.py:351
  21.6 9.2 %collective-permute-start.3 = (f32[64,1024]{1,0:T(8,128)S(1)}, f32[64,1024]{1,0:T(8,128)S(1)}, u32[]{:S(2)}, u32[]{:S(2)}) collective-permute-start(f32[64,1024]{1,0:T(8,128)S(1)} %get-tuple-element.40), channel_id=1, source_target_pairs={{0,16},{4,20},{8,24},{12,28},{16,0},{20,4},{24,8},{28,12},{32,48},... | collective-permute-start | bytes 786440 | tf_op jit(solution)/shard_map/ppermute | solution.py:351
  23.9 6.9 %collective-permute-start.2 = (f32[32,1024]{1,0:T(8,128)S(1)}, f32[32,1024]{1,0:T(8,128)S(1)}, u32[]{:S(2)}, u32[]{:S(2)}) collective-permute-start(f32[32,1024]{1,0:T(8,128)S(1)} %get-tuple-element.39.refs_4_), channel_id=1, source_target_pairs={{0,8},{4,12},{8,0},{12,4},{16,24},{20,28},{24,16},{28,20},{32,40},... | collective-permute-start | bytes 393224 | tf_op jit(solution)/shard_map/ppermute | solution.py:351
  30.8 10.2 %collective-permute-start.5 = (f32[256,1024]{1,0:T(8,128)S(1)}, f32[256,1024]{1,0:T(8,128)S(1)}, u32[]{:S(2)}, u32[]{:S(2)}) collective-permute-start(f32[256,1024]{1,0:T(8,128)S(1)} %shard_map.96.own), channel_id=1, source_target_pairs={{0,4},{4,0},{8,12},{12,8},{16,20},{20,16},{24,28},{28,24},{32,36},... | collective-permute-start | bytes 3145736 | tf_op jit(solution)/shard_map/ppermute | solution.py:351
  37.2 17.1 %copy-start.1 = (f32[512]{0:T(512)S(1)}, f32[512]{0:T(512)}, u32[]{:S(2)}) copy-start(f32[512]{0:T(512)} %param.11) | copy-start | bytes 6148
  37.2 3.8 %collective-permute-start = (f32[128,1024]{1,0:T(8,128)S(1)}, f32[128,1024]{1,0:T(8,128)S(1)}, u32[]{:S(2)}, u32[]{:S(2)}) collective-permute-start(f32[128,1024]{1,0:T(8,128)S(1)} %get-tuple-element.35), channel_id=1, source_target_pairs={{0,4},{4,0},{8,12},{12,8},{16,20},{20,16},{24,28},{28,24},{32,36},... | collective-permute-start | bytes 1572872 | tf_op jit(solution)/shard_map/ppermute | solution.py:351
  61.8 6.3 %collective-permute-start.7 = (f32[256,1024]{1,0:T(8,128)}, f32[256,1024]{1,0:T(8,128)S(1)}, u32[]{:S(2)}, u32[]{:S(2)}) collective-permute-start(f32[256,1024]{1,0:T(8,128)} %get-tuple-element.51), channel_id=1, source_target_pairs={{0,4},{4,0},{8,12},{12,8},{16,20},{20,16},{24,28},{28,24},{32,36},... | collective-permute-start | bytes 3145736 | tf_op jit(solution)/shard_map/ppermute | solution.py:351
  80.7 23.7 %all-to-all-start.3 = ((f32[4,16,1024]{2,1,0:T(8,128)}), f32[4,16,1024]{2,1,0:T(8,128)S(1)}, u32[]{:S(2)}, u32[]{:S(2)}) async-start(f32[4,16,1024]{2,1,0:T(8,128)} %shard_map.100), calls=%async_computation.3 | async-start | bytes 524288 | tf_op jit(solution)/shard_map/all_to_all | solution.py:354
  84.1 13.5 %collective-permute-start.6 = (f32[128,1024]{1,0:T(8,128)}, f32[128,1024]{1,0:T(8,128)S(1)}, u32[]{:S(2)}, u32[]{:S(2)}) collective-permute-start(f32[128,1024]{1,0:T(8,128)} %get-tuple-element.49), channel_id=1, source_target_pairs={{0,4},{4,0},{8,12},{12,8},{16,20},{20,16},{24,28},{28,24},{32,36},... | collective-permute-start | bytes 1572872 | tf_op jit(solution)/shard_map/ppermute | solution.py:351
  88.0 16.3 %collective-permute-start.8 = (f32[64,1024]{1,0:T(8,128)S(1)}, f32[64,1024]{1,0:T(8,128)S(1)}, u32[]{:S(2)}, u32[]{:S(2)}) collective-permute-start(f32[64,1024]{1,0:T(8,128)S(1)} %get-tuple-element.52), channel_id=1, source_target_pairs={{0,8},{4,12},{8,0},{12,4},{16,24},{20,28},{24,16},{28,20},{32,40},... | collective-permute-start | bytes 786440 | tf_op jit(solution)/shard_map/ppermute | solution.py:351
  90.2 11.0 %collective-permute-start.9 = (f32[32,1024]{1,0:T(8,128)S(1)}, f32[32,1024]{1,0:T(8,128)S(1)}, u32[]{:S(2)}, u32[]{:S(2)}) collective-permute-start(f32[32,1024]{1,0:T(8,128)S(1)} %get-tuple-element.53), channel_id=1, source_target_pairs={{0,16},{4,20},{8,24},{12,28},{16,0},{20,4},{24,8},{28,12},{32,48},... | collective-permute-start | bytes 393224 | tf_op jit(solution)/shard_map/ppermute | solution.py:351
  93.9 10.4 %collective-permute-start.10 = (f32[32,1024]{1,0:T(8,128)S(1)}, f32[32,1024]{1,0:T(8,128)S(1)}, u32[]{:S(2)}, u32[]{:S(2)}) collective-permute-start(f32[32,1024]{1,0:T(8,128)S(1)} %get-tuple-element.54), channel_id=1, source_target_pairs={{0,24},{4,28},{8,16},{12,20},{16,8},{20,12},{24,0},{28,4},{32,56},... | collective-permute-start | bytes 393224 | tf_op jit(solution)/shard_map/ppermute | solution.py:351

commit v2 on v1

--- a/solution.py
+++ b/solution.py
@@ -17,9 +17,8 @@
 
 L45 = ((16, 4), (16, 5))
 GATHERED = ((64, 2),) + L45 + ((32, 3),) + L45 + ((32, 3),) + L45 + L45
-LEVELS = ((256, 0), (128, 1)) + GATHERED + GATHERED
+CLOSE = ((256, 0), (128, 1))
 NEAR = 256
-KEYS = sum(rows for rows, _ in LEVELS)
 
 VM = pl.BlockSpec(memory_space=pltpu.VMEM)
 HB = pl.BlockSpec(memory_space=pltpu.HBM)
@@ -33,7 +32,7 @@
 
 def call(body, out, args, spaces="", scratch=(), grant=16):
     spaces = spaces.ljust(len(args))
-    kinds = {"s": pltpu.SMEM, "h": pltpu.HBM, " ": pltpu.VMEM}
+    kinds = {"h": pltpu.HBM, " ": pltpu.VMEM}
     args = [pltpu.with_memory_space_constraint(x, pltpu.HBM) if c == "h" else x for x, c in zip(args, spaces)]
     return pl.pallas_call(
         body,
@@ -102,8 +101,8 @@
             l4[j, :, to] = four
 
 
-def route_body(zpos, z_in, l3, c0, y23, buf):
-    z = zpos[0]
+def route_body(z_in, l3, c0, y23, buf):
+    z = (lax.axis_index("seq") >> 3) & 3
     c0[0:16, :] = z_in[z ^ 1]
     for h in range(8):
         to = slice(h * HD, (h + 1) * HD)
@@ -175,50 +174,65 @@
     return slice(h * HD, (h + 1) * HD)
 
 
-def gather(near, refs, at):
-    return jnp.concatenate([near] + [ref[:, at] for ref in refs], axis=0)
-
-
-def near_body(q_hbm, k_hbm, v_hbm, ct_hbm, q, k, v, ct, s_out, sem):
+def attend(h, q_ref, keys, values, levels):
+    query = q_ref[:, head_cols(h)] * (INV_ROOT * LOG2E)
+    s = jnp.concatenate([scores(part, query) for part in keys], axis=0)
+    parts = []
+    row = 0
+    for rows, level in levels:
+        seg = s[row : row + rows]
+        parts.append(seg + float(level) if level else seg)
+        row += rows
+    s = jnp.concatenate(parts, axis=0)
+    top = jnp.max(s, axis=0, keepdims=True)
+    e = jnp.exp2(s - top)
+    eh, el = split2(e)
+    return e, top, jnp.sum(e, axis=0, keepdims=True), dot_tn(jnp.concatenate(values, axis=0), eh, el)
+
+
+def near_body(q_hbm, k_hbm, v_hbm, ct_hbm, one, q, k, v, ct, e_out, stat, acc, sem):
     copies = []
     for i, (src, dst) in enumerate(((q_hbm, q), (k_hbm, k), (v_hbm, v), (ct_hbm, ct))):
         copies.append(pltpu.make_async_copy(src, dst, sem.at[i]))
         copies[i].start()
-    copies[0].wait()
-    copies[1].wait()
-    for h in range(4):
-        at = head_cols(h)
-        s_out[h] = scores(k[:, at], q[:, at] * (INV_ROOT * LOG2E))
-    copies[2].wait()
+    for copy in copies[:3]:
+        copy.wait()
+    for h in range(4):
+        at, vat = head_cols(h), head_cols(4 + h)
+        e, top, total, out = attend(h, q, (k[:, at], one[:, at]), (v[:, at], one[:, vat]), CLOSE)
+        e_out[h] = e
+        stat[h : h + 1, :] = top
+        stat[4 + h : 5 + h, :] = total
+        acc[h] = out
     copies[3].wait()
 
 
-def forward_body(q_ref, k_ref, v_ref, ct, one, own, peer, gain, s_near, p_out, att, send):
-    far = (one, own, peer)
-    for h in range(4):
-        at = head_cols(h)
-        query = q_ref[:, at] * (INV_ROOT * LOG2E)
-        vat = head_cols(4 + h)
-        blocks = [s_near[h]] + [scores(ref[:, at], query) for ref in far]
-        s = jnp.concatenate(blocks, axis=0)
-        parts = []
-        row = 0
-        for rows, level in LEVELS:
-            seg = s[row : row + rows]
-            parts.append(seg + float(level) if level else seg)
-            row += rows
-        s = jnp.concatenate(parts, axis=0)
-        top = jnp.max(s, axis=0, keepdims=True)
-        e = jnp.exp2(s - top)
-        p = e * (1.0 / jnp.sum(e, axis=0, keepdims=True))
-        p_out[h] = p
-        values = gather(v_ref[:, at], far, vat)
-        ph, pl_ = split2(p)
-        att[:, at] = dot_tn(values, ph, pl_).T
+def own_body(q, own, e_out, stat, acc):
+    for h in range(4):
+        at, vat = head_cols(h), head_cols(4 + h)
+        e, top, total, out = attend(h, q, (own[:, at],), (own[:, vat],), GATHERED)
+        e_out[h] = e
+        stat[h : h + 1, :] = top
+        stat[4 + h : 5 + h, :] = total
+        acc[h] = out
+
+
+def forward_body(q, peer, stat0, acc0, stat1, acc1, ct, gain, e_out, scale, att, send):
+    for h in range(4):
+        at, vat = head_cols(h), head_cols(4 + h)
+        e, top, total, out = attend(h, q, (peer[:, at],), (peer[:, vat],), GATHERED)
+        e_out[h] = e
+        top0, top1 = stat0[h : h + 1, :], stat1[h : h + 1, :]
+        most = jnp.maximum(jnp.maximum(top0, top1), top)
+        w0, w1, w2 = jnp.exp2(top0 - most), jnp.exp2(top1 - most), jnp.exp2(top - most)
+        over = 1.0 / (w0 * stat0[4 + h : 5 + h, :] + w1 * stat1[4 + h : 5 + h, :] + w2 * total)
+        w0, w1, w2 = w0 * over, w1 * over, w2 * over
+        scale[h : h + 1, :] = w0
+        scale[4 + h : 5 + h, :] = w1
+        scale[8 + h : 9 + h, :] = w2
+        att[:, at] = (acc0[h] * w0 + acc1[h] * w1 + out * w2).T
     a = att[...]
-    width = 4 * HD
-    total = jnp.sum(a, axis=1, keepdims=True)
-    mean = total * (1.0 / width)
+    mean = jnp.sum(a, axis=1, keepdims=True) * (1.0 / (4 * HD))
     away = a - mean
     sg = ct[...] * gain[...]
     lane = lax.broadcasted_iota(jnp.int32, (NEAR, HD), 1)
@@ -234,21 +248,18 @@
         send[j] = rows
 
 
+def pull(query, keys, values, e, weight, g, dot_row):
+    p = e if weight is None else e * weight
+    ph, pl_ = split2(p)
+    ds = p * (dot_nt(values, g * INV_ROOT) - dot_row)
+    sh, sl = split2(ds)
+    return dot_tn(keys, sh, sl), dot_nn(sh, sl, query), dot_nn(ph, pl_, g)
+
+
 def backward_body(
-    q_ref, k_ref, v_ref, ct, one, own, peer, gain, bias, p_in, att, got,
-    normed, dq, dv, d_one, dk, d_own, d_peer, out_buf, out_sem,
+    q, own, peer, ct, gain, att, got, e_own, e_peer, scale,
+    d_own, d_peer, dq_part, g_out, hat_out, dots,
 ):
-    written = []
-
-    def write(i, h, ref, value, col=None):
-        rows = value.shape[0]
-        out_buf[i, h, 0:rows, :] = value
-        to = ref.at[:, pl.ds((h if col is None else col) * HD, HD)]
-        copy = pltpu.make_async_copy(out_buf.at[i, h, pl.ds(0, rows)], to, out_sem.at[i, h])
-        copy.start()
-        written.append(copy)
-
-    far = (one, own, peer)
     stat = [got[j] for j in range(4)]
     mean = (stat[0][0:1] + stat[1][0:1] + stat[2][0:1] + stat[3][0:1]) * 0.25
     square = jnp.zeros_like(mean)
@@ -267,38 +278,59 @@
         table = jnp.where(sub == j, value, table)
     cols = table.T
     mean, inv, total, cross = (cols[:, j : j + 1] for j in range(4))
+    lane = lax.broadcasted_iota(jnp.int32, (NEAR, HD), 1)
+    table = jnp.zeros((NEAR, HD), F32)
     for h in range(4):
         at = head_cols(h)
-        vat = head_cols(4 + h)
-        hat = (att[:, at] - mean) * inv
-        write(0, h, normed, hat * gain[:, at] + bias[:, at])
+        mine = att[:, at]
+        hat = (mine - mean) * inv
+        hat_out[:, at] = hat
         g = inv * (ct[:, at] * gain[:, at] - total - hat * cross)
-        p = p_in[h]
-        values = gather(v_ref[:, at], far, vat)
-        keys = gather(k_ref[:, at], far, at)
-        dp = dot_nt(values, g * INV_ROOT)
-        ph, pl_ = split2(p)
-        dval = dot_nn(ph, pl_, g)
-        write(2, h, dv, dval[0:256])
-        ds = p * (dp - jnp.sum(p * dp, axis=0, keepdims=True))
-        sh, sl = split2(ds)
-        dkey = dot_nn(sh, sl, q_ref[:, at])
-        write(1, h, dq, dot_tn(keys, sh, sl).T)
+        g_out[:, at] = g
+        table = jnp.where(lane == h, jnp.sum(g * mine, axis=1, keepdims=True), table)
+    rows = table.T[0:8] * INV_ROOT
+    dots[...] = rows
+    for h in range(4):
+        at, vat = head_cols(h), head_cols(4 + h)
+        p_weight = jnp.concatenate(
+            (e_own[h] * scale[4 + h : 5 + h, :], e_peer[h] * scale[8 + h : 9 + h, :]), axis=0
+        )
+        keys = jnp.concatenate((own[:, at], peer[:, at]), axis=0)
+        values = jnp.concatenate((own[:, vat], peer[:, vat]), axis=0)
+        dq, dkey, dval = pull(q[:, at], keys, values, p_weight, None, g_out[:, at], rows[h : h + 1])
+        dq_part[:, at] = dq.T
+        d_own[:, at] = dkey[0:256]
+        d_own[:, vat] = dval[0:256]
+        d_peer[:, at] = dkey[256:512]
+        d_peer[:, vat] = dval[256:512]
+
+
+def tail_body(
+    q, k, v, one, gain, bias, e_near, scale, g, hat, dots, dq_part,
+    normed, dq_out, dk, dv, d_one, buf, sem,
+):
+    copies = [pltpu.make_async_copy(buf.at[i], (normed, dq_out)[i], sem.at[i]) for i in range(2)]
+    buf[0] = hat[...] * gain[...] + bias[...]
+    copies[0].start()
+    for h in range(4):
+        at, vat = head_cols(h), head_cols(4 + h)
+        keys = jnp.concatenate((k[:, at], one[:, at]), axis=0)
+        values = jnp.concatenate((v[:, at], one[:, vat]), axis=0)
+        dq, dkey, dval = pull(
+            q[:, at], keys, values, e_near[h], scale[h : h + 1, :], g[:, at], dots[h : h + 1, :]
+        )
+        buf[1, :, at] = dq_part[:, at] + dq.T
         dk[:, at] = dkey[0:256]
-        write(3, h, d_one, dkey[256:384])
-        write(4, h, d_one, dval[256:384], 4 + h)
-        row = NEAR + 128
-        for ref in (d_own, d_peer):
-            n = ref.shape[0]
-            ref[:, at] = dkey[row : row + n]
-            ref[:, vat] = dval[row : row + n]
-            row += n
-    for copy in written:
+        dv[:, at] = dval[0:256]
+        d_one[:, at] = dkey[256:384]
+        d_one[:, vat] = dval[256:384]
+    copies[1].start()
+    for copy in copies:
         copy.wait()
 
 
-def sum_body(ypos, mine, got, g1, g2, g3, gb):
-    y = ypos[0]
+def sum_body(mine, got, g1, g2, g3, gb):
+    y = (lax.axis_index("seq") >> 1) & 3
 
     def both(row, n):
         return mine[row : row + n, :] + got[row : row + n, :]
@@ -312,8 +344,8 @@
     gb[y] = both(224, 32)
 
 
-def unroute_body(zpos, y_in, send, buf):
-    z = zpos[0]
+def unroute_body(y_in, send, buf):
+    z = (lax.axis_index("seq") >> 3) & 3
     g = (y_in[0] + y_in[1]) + (y_in[2] + y_in[3])
     send[z] = jnp.zeros((16, 8 * HD), F32)
     send[z ^ 1] = g[0:16]
@@ -323,9 +355,8 @@
             send[z ^ j, :, to] = doubled(g[8 * j : 8 * j + 8, to], buf.at[2 * h + j - 2])
 
 
-def finish_body(zpos, dk0, dv0, got, y1a, y2, y3, z_in, dk, dv, near, sem, s3, s2, s1, s0):
-    staged = Staged((dv0,), near, sem)
-    z = zpos[0]
+def finish_body(dk0, dv0, got, y1a, y2, y3, z_in, dk, dv, s3, s2, s1, s0):
+    z = (lax.axis_index("seq") >> 3) & 3
     for h in range(8):
         to = slice(h * HD, (h + 1) * HD)
         part = z_in[z ^ 1, :, to] + (z_in[z ^ 2, :, to] + z_in[z ^ 3, :, to])
@@ -333,17 +364,12 @@
         part = doubled(part, s2.at[h]) + y1a[:, to]
         part = doubled(part, s1.at[h]) + got[:, to]
         at = head_cols(h % 4)
-        part = doubled(part, s0.at[h])
-        if h < 4:
-            dk[:, at] = dk0[:, at] + part
-        else:
-            dv[:, at] = staged.at(0, h % 4) + part
+        src, dst = (dk0, dk) if h < 4 else (dv0, dv)
+        dst[:, at] = src[:, at] + doubled(part, s0.at[h])
 
 
 def body(query, key, value, cotangent, gain, bias):
     seq = lax.axis_size("seq")
-    zpos = (lax.axis_index("seq") // 8 % 4).reshape(1).astype(jnp.int32)
-    ypos = (lax.axis_index("seq") // 2 % 4).reshape(1).astype(jnp.int32)
     z_groups = [[zh * 32 + zl * 8 + r for zl in range(4)] for zh in range(seq // 32) for r in range(8)]
     y_groups = [[z * 8 + y * 2 + c for y in range(4)] for z in range(seq // 8) for c in range(2)]
 
@@ -366,52 +392,57 @@
     y1 = swap(l2, 2)
     one = swap(l1, 1)
     c0, y23 = call(
-        route_body, (shape(32, 1024), shape(64, 1024)), (zpos, z_in, l3), "s", buffers(16, 16)
+        route_body, (shape(32, 1024), shape(64, 1024)), (z_in, l3), scratch=buffers(16, 16)
     )
     y2 = swap(y23, 4)
     y3 = swap(y23, 6)
     c1 = swap(c0, 2)
     own = call(pack_body, shape(256, 1024), (y1, c1, y2, y3, c0))
     peer = swap(own, 1)
-    q, k, v, ct, s_near = call(
+    partial = (shape(8, NEAR), shape(4, HD, NEAR))
+    q, k, v, ct, e_near, stat0, acc0 = call(
         near_body,
-        (shape(256, 512),) * 4 + (shape(4, NEAR, NEAR),),
-        (query, key, value, cotangent),
+        (shape(256, 512),) * 4 + (shape(4, 384, NEAR),) + partial,
+        (query, key, value, cotangent, one),
         "hhhh",
         [pltpu.SemaphoreType.DMA((4,))],
     )
-    inputs = (q, k, v, ct, one, own, peer, gain)
-    p, att, send = call(
-        forward_body, (shape(4, KEYS, NEAR), shape(256, 512), shape(4, 8, 256)), inputs + (s_near,)
+    e_own, stat1, acc1 = call(own_body, (shape(4, 256, NEAR),) + partial, (q, own))
+    e_peer, scale, att, send = call(
+        forward_body,
+        (shape(4, 256, NEAR), shape(16, NEAR), shape(256, 512), shape(4, 8, 256)),
+        (q, peer, stat0, acc0, stat1, acc1, ct, gain),
     )
     got = lax.all_to_all(send, "head", 0, 0, tiled=True)
-    normed, dq, dv0, d_one, dk0, d_own, d_peer = call(
+    d_own, d_peer, dq_part, g, hat, dots = call(
         backward_body,
-        (pltpu.HBM((256, 512), F32),) * 3
-        + (pltpu.HBM((128, 1024), F32), shape(256, 512), shape(256, 1024), shape(256, 1024)),
-        inputs + (bias, p, att, got),
-        scratch=staging(5),
+        (shape(256, 1024),) * 2 + (shape(256, 512),) * 3 + (shape(8, NEAR),),
+        (q, own, peer, ct, gain, att, got, e_own, e_peer, scale),
+    )
+    normed, dq, dk0, dv0, d_one = call(
+        tail_body,
+        (pltpu.HBM((256, 512), F32),) * 2 + (shape(256, 512),) * 2 + (shape(128, 1024),),
+        (q, k, v, one, gain, bias, e_near, scale, g, hat, dots, dq_part),
+        scratch=[pltpu.VMEM((2, 256, 512), F32), pltpu.SemaphoreType.DMA((2,))],
     )
     d_got = swap(d_peer, 1)
     g1, g2, g3, gb = call(
         sum_body,
         (shape(64, 1024), shape(32, 1024), shape(32, 1024), shape(4, 32, 1024)),
-        (ypos, d_own, d_got),
-        "s",
+        (d_own, d_got),
     )
     y_got = exchange(gb, y_groups)
     r1 = swap(g1, 2)
     r2 = swap(g2, 4)
     r3 = swap(g3, 6)
-    z_send = call(unroute_body, shape(4, 16, 1024), (zpos, y_got), "s", buffers(16, 16))
+    z_send = call(unroute_body, shape(4, 16, 1024), (y_got,), scratch=buffers(16, 16))
     z_got = exchange(z_send, z_groups)
     got_one = swap(d_one, 1)
     dk, dv = call(
         finish_body,
         (shape(256, 512), shape(256, 512)),
-        (zpos, dk0, dv0, got_one, r1, r2, r3, z_got),
-        "s h",
-        staging(1) + buffers(8, 32, 64, 128, 256),
+        (dk0, dv0, got_one, r1, r2, r3, z_got),
+        scratch=buffers(8, 32, 64, 128, 256),
     )
     return normed, dq, dk, dv
 

time: 107 us -> 116 us (1.084)
  local copies, waits for them, and re-layouts: 0.01 us -> 7.88 us
  waiting for transfers between devices: 16.3 us -> 18 us
    unnamed x4 -> x40, local copies, waits for them, and re-layouts: 0.01 us -> 7.88 us
    ppermute x11, waiting for transfers between devices: 13.9 us -> 15.6 us  [swap(): return lax.ppermute(x, 'seq', [(i, i ^ mask) for i in range(seq)])]
    pallas_call x9 -> x11, Pallas kernels: 19.9 us -> 19.3 us  [call(): pl.pallas_call(body, out_shape=out, in_specs=[pl.BlockSpec(memory_space=k...]
  transfers between devices with their start and end apart: 13 -> 13, of which waited for: 5 -> 6; matrix products, arithmetic and copies ran while one was open for 0% -> 0% of each run, Pallas kernels for 2% -> 7%
where the time goes in v2:
time: 116 us; the launch traced here: 115 us
  starting transfers between devices  49.2 us (42%)
  blocking collectives  19.9 us (17%)
  Pallas kernels  19.3 us (17%)
  waiting for transfers between devices  18 us (16%)
  local copies, waits for them, and re-layouts  7.88 us (7%)
    ppermute x11, starting transfers between devices, swap(): return lax.ppermute(x, 'seq', [(i, i ^ mask) for i in range(seq)])  39.2 us
    pallas_call x11, Pallas kernels, call(): pl.pallas_call(body, out_shape=out, in_specs=[pl.BlockSpec(memory_space=k...  19.3 us
    ppermute x11, waiting for transfers between devices, swap(): return lax.ppermute(x, 'seq', [(i, i ^ mask) for i in range(seq)])  15.6 us
    all_to_all x1, blocking collectives, exchange(): return lax.all_to_all(x, 'seq', 0, 0, axis_index_groups=groups, tiled=True)  11.8 us
    all_to_all x2, starting transfers between devices, exchange(): return lax.all_to_all(x, 'seq', 0, 0, axis_index_groups=groups, tiled=True)  10 us
    all_to_all x1, blocking collectives, body(): got = lax.all_to_all(send, 'head', 0, 0, tiled=True)  8.11 us
    unnamed x40, local copies, waits for them, and re-layouts  7.88 us
    all_to_all x2, waiting for transfers between devices, exchange(): return lax.all_to_all(x, 'seq', 0, 0, axis_index_groups=groups, tiled=True)  2.43 us
  transfers between devices with their start and end apart: 13, of which 6 were waited for; matrix products, arithmetic and copies ran while one was open for 0% of the time, Pallas kernels for 7%

profile of v2, /device:TPU:1, one launch (start us, length us, event | category | flops | bytes accessed | tf_op | source)
XLA Modules:
  0.0 115.2 jit_solution(1819979066573594979)
XLA Ops:
  0.6 2.3 %shard_map.93 = (f32[128,1024]{1,0:T(8,128)S(1)}, f32[64,1024]{1,0:T(8,128)S(1)}, f32[32,1024]{1,0:T(8,128)S(1)}, f32[4,16,1024]{2,1,0:T(8,128)}) custom-call(f32[256,512]{1,0:T(8,128)} %k_hbm.3, f32[256,512]{1,0:T(8,128)} %v_hbm.3), custom_call_target="tpu_custom_call" | custom-call | tf_op jit(solution)/shard_map/pallas_call | solution.py:37
  2.9 6.4 %all-to-all-start = ((f32[4,16,1024]{2,1,0:T(8,128)}), f32[4,16,1024]{2,1,0:T(8,128)S(1)}, u32[]{:S(2)}, u32[]{:S(2)}) async-start(f32[4,16,1024]{2,1,0:T(8,128)} %get-tuple-element.47), calls=%async_computation | async-start | bytes 524288 | tf_op jit(solution)/shard_map/all_to_all | solution.py:380
  9.3 3.2 %collective-permute-start.1 = (f32[64,1024]{1,0:T(8,128)S(1)}, f32[64,1024]{1,0:T(8,128)S(1)}, u32[]{:S(2)}, u32[]{:S(2)}) collective-permute-start(f32[64,1024]{1,0:T(8,128)S(1)} %get-tuple-element.46), channel_id=1, source_target_pairs={{0,8},{4,12},{8,0},{12,4},{16,24},{20,28},{24,16},{28,20},{32,40},... | collective-permute-start | bytes 786440 | tf_op jit(solution)/shard_map/ppermute | solution.py:377
  12.5 2.4 %all-to-all-done.z_in = f32[4,16,1024]{2,1,0:T(8,128)S(1)} async-done(((f32[4,16,1024]{2,1,0:T(8,128)}), f32[4,16,1024]{2,1,0:T(8,128)S(1)}, u32[]{:S(2)}, u32[]{:S(2)}) %all-to-all-start) | async-done | bytes 262176 | tf_op jit(solution)/shard_map/all_to_all | solution.py:380
  15.0 6.6 %collective-permute-start.4 = (f32[64,1024]{1,0:T(8,128)S(1)}, f32[64,1024]{1,0:T(8,128)S(1)}, u32[]{:S(2)}, u32[]{:S(2)}) collective-permute-start(f32[64,1024]{1,0:T(8,128)S(1)} %get-tuple-element.50), channel_id=1, source_target_pairs={{0,24},{4,28},{8,16},{12,20},{16,8},{20,12},{24,0},{28,4},{32,56},... | collective-permute-start | bytes 786440 | tf_op jit(solution)/shard_map/ppermute | solution.py:377
  21.6 2.3 %collective-permute-start.3 = (f32[64,1024]{1,0:T(8,128)S(1)}, f32[64,1024]{1,0:T(8,128)S(1)}, u32[]{:S(2)}, u32[]{:S(2)}) collective-permute-start(f32[64,1024]{1,0:T(8,128)S(1)} %get-tuple-element.50), channel_id=1, source_target_pairs={{0,16},{4,20},{8,24},{12,28},{16,0},{20,4},{24,8},{28,12},{32,48},... | collective-permute-start | bytes 786440 | tf_op jit(solution)/shard_map/ppermute | solution.py:377
  23.9 2.1 %collective-permute-start.2 = (f32[32,1024]{1,0:T(8,128)S(1)}, f32[32,1024]{1,0:T(8,128)S(1)}, u32[]{:S(2)}, u32[]{:S(2)}) collective-permute-start(f32[32,1024]{1,0:T(8,128)S(1)} %get-tuple-element.49.refs_4_), channel_id=1, source_target_pairs={{0,8},{4,12},{8,0},{12,4},{16,24},{20,28},{24,16},{28,20},{32,40},... | collective-permute-start | bytes 393224 | tf_op jit(solution)/shard_map/ppermute | solution.py:377
  26.0 0.0 collective-permute-done.1.refs_0_
  26.0 4.7 %collective-permute-done.2.refs_1_ = f32[32,1024]{1,0:T(8,128)S(1)} collective-permute-done((f32[32,1024]{1,0:T(8,128)S(1)}, f32[32,1024]{1,0:T(8,128)S(1)}, u32[]{:S(2)}, u32[]{:S(2)}) %collective-permute-start.2) | collective-permute-done | bytes 131104 | tf_op jit(solution)/shard_map/ppermute | solution.py:377
  30.8 0.0 collective-permute-done.4.refs_3_
  30.8 0.0 collective-permute-done.3.refs_2_
  30.8 0.1 shard_map.96.own
  30.8 6.3 %collective-permute-start.5 = (f32[256,1024]{1,0:T(8,128)S(1)}, f32[256,1024]{1,0:T(8,128)S(1)}, u32[]{:S(2)}, u32[]{:S(2)}) collective-permute-start(f32[256,1024]{1,0:T(8,128)S(1)} %shard_map.96.own), channel_id=1, source_target_pairs={{0,4},{4,0},{8,12},{12,8},{16,20},{20,16},{24,28},{28,24},{32,36},... | collective-permute-start | bytes 3145736 | tf_op jit(solution)/shard_map/ppermute | solution.py:377
  37.2 0.0 copy-start.12
  37.2 1.9 %collective-permute-start = (f32[128,1024]{1,0:T(8,128)S(1)}, f32[128,1024]{1,0:T(8,128)S(1)}, u32[]{:S(2)}, u32[]{:S(2)}) collective-permute-start(f32[128,1024]{1,0:T(8,128)S(1)} %get-tuple-element.41), channel_id=1, source_target_pairs={{0,4},{4,0},{8,12},{12,8},{16,20},{20,16},{24,28},{28,24},{32,36},... | collective-permute-start | bytes 1572872 | tf_op jit(solution)/shard_map/ppermute | solution.py:377
  39.1 1.9 %collective-permute-done.one = f32[128,1024]{1,0:T(8,128)S(1)} collective-permute-done((f32[128,1024]{1,0:T(8,128)S(1)}, f32[128,1024]{1,0:T(8,128)S(1)}, u32[]{:S(2)}, u32[]{:S(2)}) %collective-permute-start) | collective-permute-done | bytes 524320 | tf_op jit(solution)/shard_map/ppermute | solution.py:377
  41.0 3.5 %shard_map.94 = (f32[256,512]{1,0:T(8,128)S(1)}, f32[256,512]{1,0:T(8,128)S(1)}, f32[256,512]{1,0:T(8,128)S(1)}, f32[256,512]{1,0:T(8,128)S(1)}, f32[4,384,256]{...) custom-call(f32[256,512]{1,0:T(8,128)} %q_hbm.1, f32[256,512]{1,0:T(8,128)} %k_hbm.3, ...), custom_call_target="tpu_custom_call" | custom-call | tf_op jit(solution)/shard_map/pallas_call | solution.py:37
  44.5 0.0 copy-start
  44.5 2.0 %shard_map.97 = (f32[4,256,256]{2,1,0:T(8,128)S(1)}, f32[8,256]{1,0:T(8,128)S(1)}, f32[4,128,256]{2,1,0:T(8,128)S(1)}) custom-call(f32[256,512]{1,0:T(8,128)S(1)} %get-tuple-element.42.q, f32[256,1024]{1,0:T(8,128)S(1)} %shard_map.96.own), custom_call_target="tpu_custom_call" | custom-call | tf_op jit(solution)/shard_map/pallas_call | solution.py:37
  46.4 0.0 collective-permute-done.5.peer
  46.5 0.0 copy-done.12
  46.5 2.3 %shard_map.98 = (f32[4,256,256]{2,1,0:T(8,128)S(1)}, f32[16,256]{1,0:T(8,128)S(1)}, f32[256,512]{1,0:T(8,128)S(1)}, f32[4,8,256]{2,1,0:T(8,128)S(1)}) custom-call(f32[256,512]{1,0:T(8,128)S(1)} %get-tuple-element.42.q, f32[256,1024]{1,0:T(8,128)S(1)} %collective-permute-done.5.peer, f32[8,256]{1,0:T(8,128)S(1)} %get-tuple-element.51.stat0, ...), custom_call_target="tpu_custom_call" | custom-call | tf_op jit(solution)/shard_map/pallas_call | solution.py:37
  48.8 0.0 copy-done
  48.8 8.1 %all_to_all.20.got = f32[4,8,256]{2,1,0:T(8,128)S(1)} all-to-all(f32[4,8,256]{2,1,0:T(8,128)S(1)} %get-tuple-element.58), channel_id=1, replica_groups=mesh['seq'=128,'head'=4] {'head'}, dimensions={0} | all-to-all | bytes 65536 | tf_op jit(solution)/shard_map/all_to_all | solution.py:416
  56.9 4.0 %shard_map.99 = (f32[256,1024]{1,0:T(8,128)S(1)}, f32[256,1024]{1,0:T(8,128)S(1)}, f32[256,512]{1,0:T(8,128)S(1)}, f32[256,512]{1,0:T(8,128)S(1)}, f32[256,512]{1,0:T(8,128)S(1)}, /*index=5*/f32[8,256]{1,0:T(8,128)S(1)}) custom-call(f32[256,512]{1,0:T(8,128)S(1)} %get-tuple-element.42.q, f32[256,1024]{1,0:T(8,128)S(1)} %shard_map.96.own, ...), custom_call_target="tpu_custom_call" | custom-call | tf_op jit(solution)/shard_map/pallas_call | solution.py:37
  60.9 0.0 copy-start.2
  60.9 0.0 copy-start.4
  60.9 0.0 copy-start.6
  60.9 3.5 %collective-permute-start.7 = (f32[256,1024]{1,0:T(8,128)S(1)}, f32[256,1024]{1,0:T(8,128)S(1)}, u32[]{:S(2)}, u32[]{:S(2)}) collective-permute-start(f32[256,1024]{1,0:T(8,128)S(1)} %get-tuple-element.71), channel_id=1, source_target_pairs={{0,4},{4,0},{8,12},{12,8},{16,20},{20,16},{24,28},{28,24},{32,36},... | collective-permute-start | bytes 3145736 | tf_op jit(solution)/shard_map/ppermute | solution.py:377
  64.4 2.3 %collective-permute-done.7.got = f32[256,1024]{1,0:T(8,128)S(1)} collective-permute-done((f32[256,1024]{1,0:T(8,128)S(1)}, f32[256,1024]{1,0:T(8,128)S(1)}, u32[]{:S(2)}, u32[]{:S(2)}) %collective-permute-start.7) | collective-permute-done | bytes 1048608 | tf_op jit(solution)/shard_map/ppermute | solution.py:377
  66.7 0.1 shard_map.101
  66.8 0.0 copy-start.16
  66.8 0.0 copy-start.18
  66.8 0.0 copy-start.14
  66.8 0.0 copy-start.13
  66.8 11.8 %all_to_all.21.y_in = f32[4,32,1024]{2,1,0:T(8,128)S(1)} all-to-all(f32[4,32,1024]{2,1,0:T(8,128)S(1)} %get-tuple-element.75), channel_id=1, replica_groups={{0,8,16,24},{4,12,20,28},{32,40,48,56},{36,44,52,60},{64,72,80,88},{68,..., dimensions={0} | all-to-all | bytes 1048576 | tf_op jit(solution)/shard_map/all_to_all | solution.py:380
  78.6 0.0 copy-done.2
  78.6 0.0 copy-done.4
  78.6 0.0 copy-done.6
  78.6 0.8 shard_map.102
  79.4 3.6 %all-to-all-start.3 = ((f32[4,16,1024]{2,1,0:T(8,128)}), f32[4,16,1024]{2,1,0:T(8,128)S(1)}, u32[]{:S(2)}, u32[]{:S(2)}) async-start(f32[4,16,1024]{2,1,0:T(8,128)} %shard_map.102), calls=%async_computation.3 | async-start | bytes 524288 | tf_op jit(solution)/shard_map/all_to_all | solution.py:380
  83.0 0.0 copy-done.13
  83.0 0.0 copy-start.1
  83.0 1.0 copy-done.1
  84.1 1.0 copy-done.3
  85.1 1.0 copy-done.5
  86.1 1.0 copy-done.7
  87.2 3.1 %shard_map.100 = (f32[256,512]{1,0:T(8,128)}, f32[256,512]{1,0:T(8,128)}, f32[256,512]{1,0:T(8,128)S(1)}, f32[256,512]{1,0:T(8,128)S(1)}, f32[128,1024]{1,0:T(8,128)S(1)}) custom-call(f32[256,512]{1,0:T(8,128)S(1)} %get-tuple-element.42.q, f32[256,512]{1,0:T(8,128)S(1)} %get-tuple-element.43.k, f32[256,512]{1,0:T(8,128)S(1)} %copy-done.1, ...), custom_call_target="tpu_custom_call" | custom-call | tf_op jit(solution)/shard_map/pallas_call | solution.py:37
  90.3 0.0 copy-start.8
  90.3 0.8 copy-done.8
  91.1 0.8 copy-done.10
  91.9 3.7 %collective-permute-start.6 = (f32[128,1024]{1,0:T(8,128)S(1)}, f32[128,1024]{1,0:T(8,128)S(1)}, u32[]{:S(2)}, u32[]{:S(2)}) collective-permute-start(f32[128,1024]{1,0:T(8,128)S(1)} %get-tuple-element.69), channel_id=1, source_target_pairs={{0,4},{4,0},{8,12},{12,8},{16,20},{20,16},{24,28},{28,24},{32,36},... | collective-permute-start | bytes 1572872 | tf_op jit(solution)/shard_map/ppermute | solution.py:377
  95.6 2.2 %collective-permute-start.8 = (f32[64,1024]{1,0:T(8,128)S(1)}, f32[64,1024]{1,0:T(8,128)S(1)}, u32[]{:S(2)}, u32[]{:S(2)}) collective-permute-start(f32[64,1024]{1,0:T(8,128)S(1)} %copy-done.15), channel_id=1, source_target_pairs={{0,8},{4,12},{8,0},{12,4},{16,24},{20,28},{24,16},{28,20},{32,40},... | collective-permute-start | bytes 786440 | tf_op jit(solution)/shard_map/ppermute | solution.py:377
  97.8 0.0 copy-done.19
  97.8 3.7 %collective-permute-start.9 = (f32[32,1024]{1,0:T(8,128)S(1)}, f32[32,1024]{1,0:T(8,128)S(1)}, u32[]{:S(2)}, u32[]{:S(2)}) collective-permute-start(f32[32,1024]{1,0:T(8,128)S(1)} %copy-done.19), channel_id=1, source_target_pairs={{0,16},{4,20},{8,24},{12,28},{16,0},{20,4},{24,8},{28,12},{32,48},... | collective-permute-start | bytes 393224 | tf_op jit(solution)/shard_map/ppermute | solution.py:377
  101.6 3.7 %collective-permute-start.10 = (f32[32,1024]{1,0:T(8,128)S(1)}, f32[32,1024]{1,0:T(8,128)S(1)}, u32[]{:S(2)}, u32[]{:S(2)}) collective-permute-start(f32[32,1024]{1,0:T(8,128)S(1)} %copy-done.17), channel_id=1, source_target_pairs={{0,24},{4,28},{8,16},{12,20},{16,8},{20,12},{24,0},{28,4},{32,56},... | collective-permute-start | bytes 393224 | tf_op jit(solution)/shard_map/ppermute | solution.py:377
  105.3 0.0 collective-permute-done.6.got
  105.3 3.5 %collective-permute-done.9.y2 = f32[32,1024]{1,0:T(8,128)S(1)} collective-permute-done((f32[32,1024]{1,0:T(8,128)S(1)}, f32[32,1024]{1,0:T(8,128)S(1)}, u32[]{:S(2)}, u32[]{:S(2)}) %collective-permute-start.9) | collective-permute-done | bytes 131104 | tf_op jit(solution)/shard_map/ppermute | solution.py:377
  108.8 3.2 %collective-permute-done.10.y3 = f32[32,1024]{1,0:T(8,128)S(1)} collective-permute-done((f32[32,1024]{1,0:T(8,128)S(1)}, f32[32,1024]{1,0:T(8,128)S(1)}, u32[]{:S(2)}, u32[]{:S(2)}) %collective-permute-start.10) | collective-permute-done | bytes 131104 | tf_op jit(solution)/shard_map/ppermute | solution.py:377
  112.0 0.0 collective-permute-done.8.y1a
  112.0 0.0 all-to-all-done.3.z_in
  112.0 1.0 copy-done.9
  113.0 1.0 copy-done.11
  114.1 1.2 %shard_map.103 = (f32[256,512]{1,0:T(8,128)}, f32[256,512]{1,0:T(8,128)}) custom-call(f32[256,512]{1,0:T(8,128)S(1)} %copy-done.9, f32[256,512]{1,0:T(8,128)S(1)} %copy-done.11, f32[128,1024]{1,0:T(8,128)S(1)} %collective-permute-done.6.got, f32[64,1024]{1,0:T(8,128)S(1)} %collective-permute-done.8.y1a, f32[32,1024]{1,0:T(8,128)S(1)} %collective-permute-done.9.y2, ...), custom_call_target="tpu_custom_call" | custom-call | tf_op jit(solution)/shard_map/pallas_call | solution.py:37
  (15 shorter events, 0.1 us)
Async XLA Ops:
  2.9 12.1 %all-to-all-start = ((f32[4,16,1024]{2,1,0:T(8,128)}), f32[4,16,1024]{2,1,0:T(8,128)S(1)}, u32[]{:S(2)}, u32[]{:S(2)}) async-start(f32[4,16,1024]{2,1,0:T(8,128)} %get-tuple-element.47), calls=%async_computation | async-start | bytes 524288 | tf_op jit(solution)/shard_map/all_to_all | solution.py:380
  9.3 16.7 %collective-permute-start.1 = (f32[64,1024]{1,0:T(8,128)S(1)}, f32[64,1024]{1,0:T(8,128)S(1)}, u32[]{:S(2)}, u32[]{:S(2)}) collective-permute-start(f32[64,1024]{1,0:T(8,128)S(1)} %get-tuple-element.46), channel_id=1, source_target_pairs={{0,8},{4,12},{8,0},{12,4},{16,24},{20,28},{24,16},{28,20},{32,40},... | collective-permute-start | bytes 786440 | tf_op jit(solution)/shard_map/ppermute | solution.py:377
  15.0 15.7 %collective-permute-start.4 = (f32[64,1024]{1,0:T(8,128)S(1)}, f32[64,1024]{1,0:T(8,128)S(1)}, u32[]{:S(2)}, u32[]{:S(2)}) collective-permute-start(f32[64,1024]{1,0:T(8,128)S(1)} %get-tuple-element.50), channel_id=1, source_target_pairs={{0,24},{4,28},{8,16},{12,20},{16,8},{20,12},{24,0},{28,4},{32,56},... | collective-permute-start | bytes 786440 | tf_op jit(solution)/shard_map/ppermute | solution.py:377
  21.6 9.2 %collective-permute-start.3 = (f32[64,1024]{1,0:T(8,128)S(1)}, f32[64,1024]{1,0:T(8,128)S(1)}, u32[]{:S(2)}, u32[]{:S(2)}) collective-permute-start(f32[64,1024]{1,0:T(8,128)S(1)} %get-tuple-element.50), channel_id=1, source_target_pairs={{0,16},{4,20},{8,24},{12,28},{16,0},{20,4},{24,8},{28,12},{32,48},... | collective-permute-start | bytes 786440 | tf_op jit(solution)/shard_map/ppermute | solution.py:377
  23.9 6.9 %collective-permute-start.2 = (f32[32,1024]{1,0:T(8,128)S(1)}, f32[32,1024]{1,0:T(8,128)S(1)}, u32[]{:S(2)}, u32[]{:S(2)}) collective-permute-start(f32[32,1024]{1,0:T(8,128)S(1)} %get-tuple-element.49.refs_4_), channel_id=1, source_target_pairs={{0,8},{4,12},{8,0},{12,4},{16,24},{20,28},{24,16},{28,20},{32,40},... | collective-permute-start | bytes 393224 | tf_op jit(solution)/shard_map/ppermute | solution.py:377
  30.8 15.6 %collective-permute-start.5 = (f32[256,1024]{1,0:T(8,128)S(1)}, f32[256,1024]{1,0:T(8,128)S(1)}, u32[]{:S(2)}, u32[]{:S(2)}) collective-permute-start(f32[256,1024]{1,0:T(8,128)S(1)} %shard_map.96.own), channel_id=1, source_target_pairs={{0,4},{4,0},{8,12},{12,8},{16,20},{20,16},{24,28},{28,24},{32,36},... | collective-permute-start | bytes 3145736 | tf_op jit(solution)/shard_map/ppermute | solution.py:377
  37.2 9.3 %copy-start.12 = (f32[512]{0:T(512)S(1)}, f32[512]{0:T(512)}, u32[]{:S(2)}) copy-start(f32[512]{0:T(512)} %param.10) | copy-start | bytes 6148
  37.2 3.8 %collective-permute-start = (f32[128,1024]{1,0:T(8,128)S(1)}, f32[128,1024]{1,0:T(8,128)S(1)}, u32[]{:S(2)}, u32[]{:S(2)}) collective-permute-start(f32[128,1024]{1,0:T(8,128)S(1)} %get-tuple-element.41), channel_id=1, source_target_pairs={{0,4},{4,0},{8,12},{12,8},{16,20},{20,16},{24,28},{28,24},{32,36},... | collective-permute-start | bytes 1572872 | tf_op jit(solution)/shard_map/ppermute | solution.py:377
  44.5 4.3 %copy-start = (f32[256,512]{1,0:T(8,128)}, f32[256,512]{1,0:T(8,128)S(1)}, u32[]{:S(2)}) copy-start(f32[256,512]{1,0:T(8,128)S(1)} %get-tuple-element.44.v) | copy-start | bytes 1572868
  60.9 17.7 %copy-start.2 = (f32[256,512]{1,0:T(8,128)}, f32[256,512]{1,0:T(8,128)S(1)}, u32[]{:S(2)}) copy-start(f32[256,512]{1,0:T(8,128)S(1)} %get-tuple-element.64.dq_part) | copy-start | bytes 1572868
  60.9 17.7 %copy-start.4 = (f32[256,512]{1,0:T(8,128)}, f32[256,512]{1,0:T(8,128)S(1)}, u32[]{:S(2)}) copy-start(f32[256,512]{1,0:T(8,128)S(1)} %get-tuple-element.61.g) | copy-start | bytes 1572868
  60.9 17.7 %copy-start.6 = (f32[256,512]{1,0:T(8,128)}, f32[256,512]{1,0:T(8,128)S(1)}, u32[]{:S(2)}) copy-start(f32[256,512]{1,0:T(8,128)S(1)} %get-tuple-element.62.hat) | copy-start | bytes 1572868
  60.9 5.7 %collective-permute-start.7 = (f32[256,1024]{1,0:T(8,128)S(1)}, f32[256,1024]{1,0:T(8,128)S(1)}, u32[]{:S(2)}, u32[]{:S(2)}) collective-permute-start(f32[256,1024]{1,0:T(8,128)S(1)} %get-tuple-element.71), channel_id=1, source_target_pairs={{0,4},{4,0},{8,12},{12,8},{16,20},{20,16},{24,28},{28,24},{32,36},... | collective-permute-start | bytes 3145736 | tf_op jit(solution)/shard_map/ppermute | solution.py:377
  66.8 11.8 %copy-start.16 = (f32[32,1024]{1,0:T(8,128)}, f32[32,1024]{1,0:T(8,128)S(1)}, u32[]{:S(2)}) copy-start(f32[32,1024]{1,0:T(8,128)S(1)} %get-tuple-element.74) | copy-start | bytes 393220
  66.8 11.8 %copy-start.18 = (f32[32,1024]{1,0:T(8,128)}, f32[32,1024]{1,0:T(8,128)S(1)}, u32[]{:S(2)}) copy-start(f32[32,1024]{1,0:T(8,128)S(1)} %get-tuple-element.73) | copy-start | bytes 393220
  66.8 12.6 %copy-start.14 = (f32[64,1024]{1,0:T(8,128)}, f32[64,1024]{1,0:T(8,128)S(1)}, u32[]{:S(2)}) copy-start(f32[64,1024]{1,0:T(8,128)S(1)} %get-tuple-element.72) | copy-start | bytes 786436
  66.8 16.2 %copy-start.13 = (f32[512]{0:T(512)S(1)}, f32[512]{0:T(512)}, u32[]{:S(2)}) copy-start(f32[512]{0:T(512)} %param.11) | copy-start | bytes 6148
  79.4 32.6 %all-to-all-start.3 = ((f32[4,16,1024]{2,1,0:T(8,128)}), f32[4,16,1024]{2,1,0:T(8,128)S(1)}, u32[]{:S(2)}, u32[]{:S(2)}) async-start(f32[4,16,1024]{2,1,0:T(8,128)} %shard_map.102), calls=%async_computation.3 | async-start | bytes 524288 | tf_op jit(solution)/shard_map/all_to_all | solution.py:380
  83.0 1.0 copy-start.1
  84.1 1.0 copy-start.3
  85.1 1.0 copy-start.5
  86.1 1.0 copy-start.7
  87.2 8.4 %copy-start.15 = (f32[64,1024]{1,0:T(8,128)S(1)}, f32[64,1024]{1,0:T(8,128)}, u32[]{:S(2)}) copy-start(f32[64,1024]{1,0:T(8,128)} %copy-done.14) | copy-start | bytes 786436
  87.2 10.7 %copy-start.19 = (f32[32,1024]{1,0:T(8,128)S(1)}, f32[32,1024]{1,0:T(8,128)}, u32[]{:S(2)}) copy-start(f32[32,1024]{1,0:T(8,128)} %copy-done.18) | copy-start | bytes 393220
  87.2 14.4 %copy-start.17 = (f32[32,1024]{1,0:T(8,128)S(1)}, f32[32,1024]{1,0:T(8,128)}, u32[]{:S(2)}) copy-start(f32[32,1024]{1,0:T(8,128)} %copy-done.16) | copy-start | bytes 393220
  90.3 0.8 copy-start.8
  91.1 0.8 copy-start.10
  91.9 13.4 %collective-permute-start.6 = (f32[128,1024]{1,0:T(8,128)S(1)}, f32[128,1024]{1,0:T(8,128)S(1)}, u32[]{:S(2)}, u32[]{:S(2)}) collective-permute-start(f32[128,1024]{1,0:T(8,128)S(1)} %get-tuple-element.69), channel_id=1, source_target_pairs={{0,4},{4,0},{8,12},{12,8},{16,20},{20,16},{24,28},{28,24},{32,36},... | collective-permute-start | bytes 1572872 | tf_op jit(solution)/shard_map/ppermute | solution.py:377
  95.6 16.3 %collective-permute-start.8 = (f32[64,1024]{1,0:T(8,128)S(1)}, f32[64,1024]{1,0:T(8,128)S(1)}, u32[]{:S(2)}, u32[]{:S(2)}) collective-permute-start(f32[64,1024]{1,0:T(8,128)S(1)} %copy-done.15), channel_id=1, source_target_pairs={{0,8},{4,12},{8,0},{12,4},{16,24},{20,28},{24,16},{28,20},{32,40},... | collective-permute-start | bytes 786440 | tf_op jit(solution)/shard_map/ppermute | solution.py:377
  97.8 10.9 %collective-permute-start.9 = (f32[32,1024]{1,0:T(8,128)S(1)}, f32[32,1024]{1,0:T(8,128)S(1)}, u32[]{:S(2)}, u32[]{:S(2)}) collective-permute-start(f32[32,1024]{1,0:T(8,128)S(1)} %copy-done.19), channel_id=1, source_target_pairs={{0,16},{4,20},{8,24},{12,28},{16,0},{20,4},{24,8},{28,12},{32,48},... | collective-permute-start | bytes 393224 | tf_op jit(solution)/shard_map/ppermute | solution.py:377
  101.6 10.4 %collective-permute-start.10 = (f32[32,1024]{1,0:T(8,128)S(1)}, f32[32,1024]{1,0:T(8,128)S(1)}, u32[]{:S(2)}, u32[]{:S(2)}) collective-permute-start(f32[32,1024]{1,0:T(8,128)S(1)} %copy-done.17), channel_id=1, source_target_pairs={{0,24},{4,28},{8,16},{12,20},{16,8},{20,12},{24,0},{28,4},{32,56},... | collective-permute-start | bytes 393224 | tf_op jit(solution)/shard_map/ppermute | solution.py:377
  112.0 1.0 copy-start.9
  113.0 1.0 copy-start.11

commit v3 on v2

--- a/solution.py
+++ b/solution.py
@@ -21,7 +21,6 @@
 NEAR = 256
 
 VM = pl.BlockSpec(memory_space=pltpu.VMEM)
-HB = pl.BlockSpec(memory_space=pltpu.HBM)
 F32 = jnp.float32
 BF16 = jnp.bfloat16
 
@@ -38,32 +37,10 @@
         body,
         out_shape=out,
         in_specs=[pl.BlockSpec(memory_space=kinds[c]) for c in spaces],
-        out_specs=jax.tree.map(lambda x: HB if isinstance(x, pl.MemoryRef) else VM, out),
+        out_specs=jax.tree.map(lambda x: pl.BlockSpec(memory_space=x.memory_space) if isinstance(x, pl.MemoryRef) else VM, out),
         scratch_shapes=scratch,
         compiler_params=pltpu.CompilerParams(vmem_limit_bytes=grant << 20),
     )(*args)
-
-
-def staging(count):
-    return [pltpu.VMEM((count, 4, NEAR, HD), F32), pltpu.SemaphoreType.DMA((count, 4))]
-
-
-class Staged:
-    def __init__(self, refs, buf, sem):
-        self.buf, self.copies = buf, {}
-        for h in range(4):
-            for i, ref in enumerate(refs):
-                copy = pltpu.make_async_copy(ref.at[:, pl.ds(h * HD, HD)], buf.at[i, h], sem.at[i, h])
-                copy.start()
-                self.copies[i, h] = copy
-
-    def wait(self, i, h):
-        if (i, h) in self.copies:
-            self.copies.pop((i, h)).wait()
-
-    def at(self, i, h):
-        self.wait(i, h)
-        return self.buf[i, h]
 
 
 def halves(value, buf):
@@ -84,13 +61,20 @@
     return [pltpu.VMEM((count, n, HD), F32) for n in rows]
 
 
-def coarsen_body(k_hbm, v_hbm, l1, l2, l3, l4, kv, sem, b1, b2, b3):
-    staged = Staged((k_hbm, v_hbm), kv, sem)
+def coarsen_body(k_hbm, v_hbm, l1, l2, l3, l4, kv, sem, b0, b1, b2, b3):
+    copies = []
+    for i, src in enumerate((k_hbm, v_hbm)):
+        for j in range(2):
+            rows = pl.ds(j * 128, 128)
+            copies.append(pltpu.make_async_copy(src.at[rows], kv.at[i, rows], sem.at[i, j]))
+            copies[-1].start()
     for h in range(8):
-        i, j = h // 4, h % 4
-        staged.wait(i, j)
+        i = h // 4
+        if h % 4 == 0:
+            copies[2 * i].wait()
+            copies[2 * i + 1].wait()
         to = slice(h * HD, (h + 1) * HD)
-        one = 0.5 * (kv[i, j, pl.ds(0, 128, stride=2), :] + kv[i, j, pl.ds(1, 128, stride=2), :])
+        one = halves(kv[i, :, head_cols(h % 4)], b0.at[h])
         l1[:, to] = one
         two = halves(one, b1.at[h])
         l2[:, to] = two
@@ -355,7 +339,8 @@
             send[z ^ j, :, to] = doubled(g[8 * j : 8 * j + 8, to], buf.at[2 * h + j - 2])
 
 
-def finish_body(dk0, dv0, got, y1a, y2, y3, z_in, dk, dv, s3, s2, s1, s0):
+def finish_body(dk0, dv0, got, y1a, y2, y3, z_in, dk, dv, out, sem, s3, s2, s1, s0):
+    written = []
     z = (lax.axis_index("seq") >> 3) & 3
     for h in range(8):
         to = slice(h * HD, (h + 1) * HD)
@@ -365,7 +350,13 @@
         part = doubled(part, s1.at[h]) + got[:, to]
         at = head_cols(h % 4)
         src, dst = (dk0, dk) if h < 4 else (dv0, dv)
-        dst[:, at] = src[:, at] + doubled(part, s0.at[h])
+        out[h // 4, :, at] = src[:, at] + doubled(part, s0.at[h])
+        if h % 2:
+            cols = pl.ds((h % 4 - 1) * HD, 2 * HD)
+            written.append(pltpu.make_async_copy(out.at[h // 4, :, cols], dst.at[:, cols], sem.at[h // 2]))
+            written[-1].start()
+    for copy in written:
+        copy.wait()
 
 
 def body(query, key, value, cotangent, gain, bias):
@@ -386,7 +377,7 @@
         (shape(128, 1024), shape(64, 1024), shape(32, 1024), shape(4, 16, 1024)),
         (key, value),
         "hh",
-        staging(2) + buffers(8, 128, 64, 32),
+        [pltpu.VMEM((2, 256, 512), F32), pltpu.SemaphoreType.DMA((2, 2))] + buffers(8, 256, 128, 64, 32),
     )
     z_in = exchange(l4, z_groups)
     y1 = swap(l2, 2)
@@ -440,9 +431,9 @@
     got_one = swap(d_one, 1)
     dk, dv = call(
         finish_body,
-        (shape(256, 512), shape(256, 512)),
+        (pltpu.HBM((256, 512), F32),) * 2,
         (dk0, dv0, got_one, r1, r2, r3, z_got),
-        scratch=buffers(8, 32, 64, 128, 256),
+        scratch=[pltpu.VMEM((2, 256, 512), F32), pltpu.SemaphoreType.DMA((4,))] + buffers(8, 32, 64, 128, 256),
     )
     return normed, dq, dk, dv
 

time: 116 us -> 116 us (level)
  no operation moved by 1% of the time
where the time goes in v3:
time: 116 us; the launch traced here: 115 us
  starting transfers between devices  49.2 us (42%)
  blocking collectives  19.9 us (17%)
  Pallas kernels  19.1 us (16%)
  waiting for transfers between devices  18 us (16%)
  local copies, waits for them, and re-layouts  7.88 us (7%)
    ppermute x11, starting transfers between devices, swap(): return lax.ppermute(x, 'seq', [(i, i ^ mask) for i in range(seq)])  39.2 us
    pallas_call x11, Pallas kernels, call(): pl.pallas_call(body, out_shape=out, in_specs=[pl.BlockSpec(memory_space=k...  19.1 us
    ppermute x11, waiting for transfers between devices, swap(): return lax.ppermute(x, 'seq', [(i, i ^ mask) for i in range(seq)])  15.6 us
    all_to_all x1, blocking collectives, exchange(): return lax.all_to_all(x, 'seq', 0, 0, axis_index_groups=groups, tiled=True)  11.8 us
    all_to_all x2, starting transfers between devices, exchange(): return lax.all_to_all(x, 'seq', 0, 0, axis_index_groups=groups, tiled=True)  10 us
    all_to_all x1, blocking collectives, body(): got = lax.all_to_all(send, 'head', 0, 0, tiled=True)  8.11 us
    unnamed x40, local copies, waits for them, and re-layouts  7.88 us
    all_to_all x2, waiting for transfers between devices, exchange(): return lax.all_to_all(x, 'seq', 0, 0, axis_index_groups=groups, tiled=True)  2.43 us
  transfers between devices with their start and end apart: 13, of which 6 were waited for; matrix products, arithmetic and copies ran while one was open for 0% of the time, Pallas kernels for 7%

profile of v3, /device:TPU:1, one launch (start us, length us, event | category | flops | bytes accessed | tf_op | source)
XLA Modules:
  0.0 115.2 jit_solution(15063384675130586034)
XLA Ops:
  0.6 2.1 %shard_map.93 = (f32[128,1024]{1,0:T(8,128)S(1)}, f32[64,1024]{1,0:T(8,128)S(1)}, f32[32,1024]{1,0:T(8,128)S(1)}, f32[4,16,1024]{2,1,0:T(8,128)}) custom-call(f32[256,512]{1,0:T(8,128)} %k_hbm.3, f32[256,512]{1,0:T(8,128)} %v_hbm.3), custom_call_target="tpu_custom_call" | custom-call | tf_op jit(solution)/shard_map/pallas_call | solution.py:36
  2.8 6.4 %all-to-all-start = ((f32[4,16,1024]{2,1,0:T(8,128)}), f32[4,16,1024]{2,1,0:T(8,128)S(1)}, u32[]{:S(2)}, u32[]{:S(2)}) async-start(f32[4,16,1024]{2,1,0:T(8,128)} %get-tuple-element.47), calls=%async_computation | async-start | bytes 524288 | tf_op jit(solution)/shard_map/all_to_all | solution.py:371
  9.2 3.2 %collective-permute-start.1 = (f32[64,1024]{1,0:T(8,128)S(1)}, f32[64,1024]{1,0:T(8,128)S(1)}, u32[]{:S(2)}, u32[]{:S(2)}) collective-permute-start(f32[64,1024]{1,0:T(8,128)S(1)} %get-tuple-element.46), channel_id=1, source_target_pairs={{0,8},{4,12},{8,0},{12,4},{16,24},{20,28},{24,16},{28,20},{32,40},... | collective-permute-start | bytes 786440 | tf_op jit(solution)/shard_map/ppermute | solution.py:368
  12.4 2.4 %all-to-all-done.z_in = f32[4,16,1024]{2,1,0:T(8,128)S(1)} async-done(((f32[4,16,1024]{2,1,0:T(8,128)}), f32[4,16,1024]{2,1,0:T(8,128)S(1)}, u32[]{:S(2)}, u32[]{:S(2)}) %all-to-all-start) | async-done | bytes 262176 | tf_op jit(solution)/shard_map/all_to_all | solution.py:371
  14.9 6.6 %collective-permute-start.4 = (f32[64,1024]{1,0:T(8,128)S(1)}, f32[64,1024]{1,0:T(8,128)S(1)}, u32[]{:S(2)}, u32[]{:S(2)}) collective-permute-start(f32[64,1024]{1,0:T(8,128)S(1)} %get-tuple-element.50), channel_id=1, source_target_pairs={{0,24},{4,28},{8,16},{12,20},{16,8},{20,12},{24,0},{28,4},{32,56},... | collective-permute-start | bytes 786440 | tf_op jit(solution)/shard_map/ppermute | solution.py:368
  21.5 2.3 %collective-permute-start.3 = (f32[64,1024]{1,0:T(8,128)S(1)}, f32[64,1024]{1,0:T(8,128)S(1)}, u32[]{:S(2)}, u32[]{:S(2)}) collective-permute-start(f32[64,1024]{1,0:T(8,128)S(1)} %get-tuple-element.50), channel_id=1, source_target_pairs={{0,16},{4,20},{8,24},{12,28},{16,0},{20,4},{24,8},{28,12},{32,48},... | collective-permute-start | bytes 786440 | tf_op jit(solution)/shard_map/ppermute | solution.py:368
  23.7 2.1 %collective-permute-start.2 = (f32[32,1024]{1,0:T(8,128)S(1)}, f32[32,1024]{1,0:T(8,128)S(1)}, u32[]{:S(2)}, u32[]{:S(2)}) collective-permute-start(f32[32,1024]{1,0:T(8,128)S(1)} %get-tuple-element.49.refs_4_), channel_id=1, source_target_pairs={{0,8},{4,12},{8,0},{12,4},{16,24},{20,28},{24,16},{28,20},{32,40},... | collective-permute-start | bytes 393224 | tf_op jit(solution)/shard_map/ppermute | solution.py:368
  25.9 0.0 collective-permute-done.1.refs_0_
  25.9 4.7 %collective-permute-done.2.refs_1_ = f32[32,1024]{1,0:T(8,128)S(1)} collective-permute-done((f32[32,1024]{1,0:T(8,128)S(1)}, f32[32,1024]{1,0:T(8,128)S(1)}, u32[]{:S(2)}, u32[]{:S(2)}) %collective-permute-start.2) | collective-permute-done | bytes 131104 | tf_op jit(solution)/shard_map/ppermute | solution.py:368
  30.6 0.0 collective-permute-done.4.refs_3_
  30.6 0.0 collective-permute-done.3.refs_2_
  30.6 0.1 shard_map.96.own
  30.7 6.3 %collective-permute-start.5 = (f32[256,1024]{1,0:T(8,128)S(1)}, f32[256,1024]{1,0:T(8,128)S(1)}, u32[]{:S(2)}, u32[]{:S(2)}) collective-permute-start(f32[256,1024]{1,0:T(8,128)S(1)} %shard_map.96.own), channel_id=1, source_target_pairs={{0,4},{4,0},{8,12},{12,8},{16,20},{20,16},{24,28},{28,24},{32,36},... | collective-permute-start | bytes 3145736 | tf_op jit(solution)/shard_map/ppermute | solution.py:368
  37.0 0.0 copy-start.12
  37.0 1.9 %collective-permute-start = (f32[128,1024]{1,0:T(8,128)S(1)}, f32[128,1024]{1,0:T(8,128)S(1)}, u32[]{:S(2)}, u32[]{:S(2)}) collective-permute-start(f32[128,1024]{1,0:T(8,128)S(1)} %get-tuple-element.41), channel_id=1, source_target_pairs={{0,4},{4,0},{8,12},{12,8},{16,20},{20,16},{24,28},{28,24},{32,36},... | collective-permute-start | bytes 1572872 | tf_op jit(solution)/shard_map/ppermute | solution.py:368
  39.0 1.9 %collective-permute-done.one = f32[128,1024]{1,0:T(8,128)S(1)} collective-permute-done((f32[128,1024]{1,0:T(8,128)S(1)}, f32[128,1024]{1,0:T(8,128)S(1)}, u32[]{:S(2)}, u32[]{:S(2)}) %collective-permute-start) | collective-permute-done | bytes 524320 | tf_op jit(solution)/shard_map/ppermute | solution.py:368
  40.8 3.5 %shard_map.94 = (f32[256,512]{1,0:T(8,128)S(1)}, f32[256,512]{1,0:T(8,128)S(1)}, f32[256,512]{1,0:T(8,128)S(1)}, f32[256,512]{1,0:T(8,128)S(1)}, f32[4,384,256]{...) custom-call(f32[256,512]{1,0:T(8,128)} %q_hbm.1, f32[256,512]{1,0:T(8,128)} %k_hbm.3, ...), custom_call_target="tpu_custom_call" | custom-call | tf_op jit(solution)/shard_map/pallas_call | solution.py:36
  44.3 0.0 copy-start
  44.3 2.0 %shard_map.97 = (f32[4,256,256]{2,1,0:T(8,128)S(1)}, f32[8,256]{1,0:T(8,128)S(1)}, f32[4,128,256]{2,1,0:T(8,128)S(1)}) custom-call(f32[256,512]{1,0:T(8,128)S(1)} %get-tuple-element.42.q, f32[256,1024]{1,0:T(8,128)S(1)} %shard_map.96.own), custom_call_target="tpu_custom_call" | custom-call | tf_op jit(solution)/shard_map/pallas_call | solution.py:36
  46.3 0.0 collective-permute-done.5.peer
  46.3 0.0 copy-done.12
  46.3 2.3 %shard_map.98 = (f32[4,256,256]{2,1,0:T(8,128)S(1)}, f32[16,256]{1,0:T(8,128)S(1)}, f32[256,512]{1,0:T(8,128)S(1)}, f32[4,8,256]{2,1,0:T(8,128)S(1)}) custom-call(f32[256,512]{1,0:T(8,128)S(1)} %get-tuple-element.42.q, f32[256,1024]{1,0:T(8,128)S(1)} %collective-permute-done.5.peer, f32[8,256]{1,0:T(8,128)S(1)} %get-tuple-element.51.stat0, ...), custom_call_target="tpu_custom_call" | custom-call | tf_op jit(solution)/shard_map/pallas_call | solution.py:36
  48.6 0.0 copy-done
  48.6 8.1 %all_to_all.20.got = f32[4,8,256]{2,1,0:T(8,128)S(1)} all-to-all(f32[4,8,256]{2,1,0:T(8,128)S(1)} %get-tuple-element.58), channel_id=1, replica_groups=mesh['seq'=128,'head'=4] {'head'}, dimensions={0} | all-to-all | bytes 65536 | tf_op jit(solution)/shard_map/all_to_all | solution.py:407
  56.8 4.0 %shard_map.99 = (f32[256,1024]{1,0:T(8,128)S(1)}, f32[256,1024]{1,0:T(8,128)S(1)}, f32[256,512]{1,0:T(8,128)S(1)}, f32[256,512]{1,0:T(8,128)S(1)}, f32[256,512]{1,0:T(8,128)S(1)}, /*index=5*/f32[8,256]{1,0:T(8,128)S(1)}) custom-call(f32[256,512]{1,0:T(8,128)S(1)} %get-tuple-element.42.q, f32[256,1024]{1,0:T(8,128)S(1)} %shard_map.96.own, ...), custom_call_target="tpu_custom_call" | custom-call | tf_op jit(solution)/shard_map/pallas_call | solution.py:36
  60.8 0.0 copy-start.2
  60.8 0.0 copy-start.4
  60.8 0.0 copy-start.6
  60.8 3.5 %collective-permute-start.7 = (f32[256,1024]{1,0:T(8,128)S(1)}, f32[256,1024]{1,0:T(8,128)S(1)}, u32[]{:S(2)}, u32[]{:S(2)}) collective-permute-start(f32[256,1024]{1,0:T(8,128)S(1)} %get-tuple-element.71), channel_id=1, source_target_pairs={{0,4},{4,0},{8,12},{12,8},{16,20},{20,16},{24,28},{28,24},{32,36},... | collective-permute-start | bytes 3145736 | tf_op jit(solution)/shard_map/ppermute | solution.py:368
  64.3 2.3 %collective-permute-done.7.got = f32[256,1024]{1,0:T(8,128)S(1)} collective-permute-done((f32[256,1024]{1,0:T(8,128)S(1)}, f32[256,1024]{1,0:T(8,128)S(1)}, u32[]{:S(2)}, u32[]{:S(2)}) %collective-permute-start.7) | collective-permute-done | bytes 1048608 | tf_op jit(solution)/shard_map/ppermute | solution.py:368
  66.5 0.1 shard_map.101
  66.6 0.0 copy-start.16
  66.7 0.0 copy-start.18
  66.7 0.0 copy-start.14
  66.7 0.0 copy-start.13
  66.7 11.8 %all_to_all.21.y_in = f32[4,32,1024]{2,1,0:T(8,128)S(1)} all-to-all(f32[4,32,1024]{2,1,0:T(8,128)S(1)} %get-tuple-element.75), channel_id=1, replica_groups={{0,8,16,24},{4,12,20,28},{32,40,48,56},{36,44,52,60},{64,72,80,88},{68,..., dimensions={0} | all-to-all | bytes 1048576 | tf_op jit(solution)/shard_map/all_to_all | solution.py:371
  78.5 0.0 copy-done.2
  78.5 0.0 copy-done.4
  78.5 0.0 copy-done.6
  78.5 0.0 copy-done.16
  78.5 0.8 shard_map.102
  79.3 3.6 %all-to-all-start.3 = ((f32[4,16,1024]{2,1,0:T(8,128)}), f32[4,16,1024]{2,1,0:T(8,128)S(1)}, u32[]{:S(2)}, u32[]{:S(2)}) async-start(f32[4,16,1024]{2,1,0:T(8,128)} %shard_map.102), calls=%async_computation.3 | async-start | bytes 524288 | tf_op jit(solution)/shard_map/all_to_all | solution.py:371
  82.9 0.0 copy-start.1
  82.9 1.0 copy-done.1
  83.9 1.0 copy-done.3
  85.0 1.0 copy-done.5
  86.0 1.0 copy-done.7
  87.0 3.1 %shard_map.100 = (f32[256,512]{1,0:T(8,128)}, f32[256,512]{1,0:T(8,128)}, f32[256,512]{1,0:T(8,128)S(1)}, f32[256,512]{1,0:T(8,128)S(1)}, f32[128,1024]{1,0:T(8,128)S(1)}) custom-call(f32[256,512]{1,0:T(8,128)S(1)} %get-tuple-element.42.q, f32[256,512]{1,0:T(8,128)S(1)} %get-tuple-element.43.k, f32[256,512]{1,0:T(8,128)S(1)} %copy-done.1, ...), custom_call_target="tpu_custom_call" | custom-call | tf_op jit(solution)/shard_map/pallas_call | solution.py:36
  90.2 0.0 copy-start.8
  90.2 0.8 copy-done.8
  91.0 0.8 copy-done.10
  91.8 3.7 %collective-permute-start.6 = (f32[128,1024]{1,0:T(8,128)S(1)}, f32[128,1024]{1,0:T(8,128)S(1)}, u32[]{:S(2)}, u32[]{:S(2)}) collective-permute-start(f32[128,1024]{1,0:T(8,128)S(1)} %get-tuple-element.69), channel_id=1, source_target_pairs={{0,4},{4,0},{8,12},{12,8},{16,20},{20,16},{24,28},{28,24},{32,36},... | collective-permute-start | bytes 1572872 | tf_op jit(solution)/shard_map/ppermute | solution.py:368
  95.5 2.2 %collective-permute-start.8 = (f32[64,1024]{1,0:T(8,128)S(1)}, f32[64,1024]{1,0:T(8,128)S(1)}, u32[]{:S(2)}, u32[]{:S(2)}) collective-permute-start(f32[64,1024]{1,0:T(8,128)S(1)} %copy-done.15), channel_id=1, source_target_pairs={{0,8},{4,12},{8,0},{12,4},{16,24},{20,28},{24,16},{28,20},{32,40},... | collective-permute-start | bytes 786440 | tf_op jit(solution)/shard_map/ppermute | solution.py:368
  97.7 0.0 copy-done.19
  97.7 3.7 %collective-permute-start.9 = (f32[32,1024]{1,0:T(8,128)S(1)}, f32[32,1024]{1,0:T(8,128)S(1)}, u32[]{:S(2)}, u32[]{:S(2)}) collective-permute-start(f32[32,1024]{1,0:T(8,128)S(1)} %copy-done.19), channel_id=1, source_target_pairs={{0,16},{4,20},{8,24},{12,28},{16,0},{20,4},{24,8},{28,12},{32,48},... | collective-permute-start | bytes 393224 | tf_op jit(solution)/shard_map/ppermute | solution.py:368
  101.4 3.7 %collective-permute-start.10 = (f32[32,1024]{1,0:T(8,128)S(1)}, f32[32,1024]{1,0:T(8,128)S(1)}, u32[]{:S(2)}, u32[]{:S(2)}) collective-permute-start(f32[32,1024]{1,0:T(8,128)S(1)} %copy-done.17), channel_id=1, source_target_pairs={{0,24},{4,28},{8,16},{12,20},{16,8},{20,12},{24,0},{28,4},{32,56},... | collective-permute-start | bytes 393224 | tf_op jit(solution)/shard_map/ppermute | solution.py:368
  105.1 0.0 collective-permute-done.6.got
  105.1 3.5 %collective-permute-done.9.y2 = f32[32,1024]{1,0:T(8,128)S(1)} collective-permute-done((f32[32,1024]{1,0:T(8,128)S(1)}, f32[32,1024]{1,0:T(8,128)S(1)}, u32[]{:S(2)}, u32[]{:S(2)}) %collective-permute-start.9) | collective-permute-done | bytes 131104 | tf_op jit(solution)/shard_map/ppermute | solution.py:368
  108.6 3.2 %collective-permute-done.10.y3 = f32[32,1024]{1,0:T(8,128)S(1)} collective-permute-done((f32[32,1024]{1,0:T(8,128)S(1)}, f32[32,1024]{1,0:T(8,128)S(1)}, u32[]{:S(2)}, u32[]{:S(2)}) %collective-permute-start.10) | collective-permute-done | bytes 131104 | tf_op jit(solution)/shard_map/ppermute | solution.py:368
  111.8 0.0 collective-permute-done.8.y1a
  111.8 0.0 all-to-all-done.3.z_in
  111.8 1.0 copy-done.9
  112.9 1.0 copy-done.11
  113.9 1.1 shard_map.103
  (15 shorter events, 0.1 us)
Async XLA Ops:
  2.8 12.1 %all-to-all-start = ((f32[4,16,1024]{2,1,0:T(8,128)}), f32[4,16,1024]{2,1,0:T(8,128)S(1)}, u32[]{:S(2)}, u32[]{:S(2)}) async-start(f32[4,16,1024]{2,1,0:T(8,128)} %get-tuple-element.47), calls=%async_computation | async-start | bytes 524288 | tf_op jit(solution)/shard_map/all_to_all | solution.py:371
  9.2 16.7 %collective-permute-start.1 = (f32[64,1024]{1,0:T(8,128)S(1)}, f32[64,1024]{1,0:T(8,128)S(1)}, u32[]{:S(2)}, u32[]{:S(2)}) collective-permute-start(f32[64,1024]{1,0:T(8,128)S(1)} %get-tuple-element.46), channel_id=1, source_target_pairs={{0,8},{4,12},{8,0},{12,4},{16,24},{20,28},{24,16},{28,20},{32,40},... | collective-permute-start | bytes 786440 | tf_op jit(solution)/shard_map/ppermute | solution.py:368
  14.9 15.7 %collective-permute-start.4 = (f32[64,1024]{1,0:T(8,128)S(1)}, f32[64,1024]{1,0:T(8,128)S(1)}, u32[]{:S(2)}, u32[]{:S(2)}) collective-permute-start(f32[64,1024]{1,0:T(8,128)S(1)} %get-tuple-element.50), channel_id=1, source_target_pairs={{0,24},{4,28},{8,16},{12,20},{16,8},{20,12},{24,0},{28,4},{32,56},... | collective-permute-start | bytes 786440 | tf_op jit(solution)/shard_map/ppermute | solution.py:368
  21.5 9.2 %collective-permute-start.3 = (f32[64,1024]{1,0:T(8,128)S(1)}, f32[64,1024]{1,0:T(8,128)S(1)}, u32[]{:S(2)}, u32[]{:S(2)}) collective-permute-start(f32[64,1024]{1,0:T(8,128)S(1)} %get-tuple-element.50), channel_id=1, source_target_pairs={{0,16},{4,20},{8,24},{12,28},{16,0},{20,4},{24,8},{28,12},{32,48},... | collective-permute-start | bytes 786440 | tf_op jit(solution)/shard_map/ppermute | solution.py:368
  23.7 6.9 %collective-permute-start.2 = (f32[32,1024]{1,0:T(8,128)S(1)}, f32[32,1024]{1,0:T(8,128)S(1)}, u32[]{:S(2)}, u32[]{:S(2)}) collective-permute-start(f32[32,1024]{1,0:T(8,128)S(1)} %get-tuple-element.49.refs_4_), channel_id=1, source_target_pairs={{0,8},{4,12},{8,0},{12,4},{16,24},{20,28},{24,16},{28,20},{32,40},... | collective-permute-start | bytes 393224 | tf_op jit(solution)/shard_map/ppermute | solution.py:368
  30.7 15.6 %collective-permute-start.5 = (f32[256,1024]{1,0:T(8,128)S(1)}, f32[256,1024]{1,0:T(8,128)S(1)}, u32[]{:S(2)}, u32[]{:S(2)}) collective-permute-start(f32[256,1024]{1,0:T(8,128)S(1)} %shard_map.96.own), channel_id=1, source_target_pairs={{0,4},{4,0},{8,12},{12,8},{16,20},{20,16},{24,28},{28,24},{32,36},... | collective-permute-start | bytes 3145736 | tf_op jit(solution)/shard_map/ppermute | solution.py:368
  37.0 9.3 %copy-start.12 = (f32[512]{0:T(512)S(1)}, f32[512]{0:T(512)}, u32[]{:S(2)}) copy-start(f32[512]{0:T(512)} %param.10) | copy-start | bytes 6148
  37.0 3.8 %collective-permute-start = (f32[128,1024]{1,0:T(8,128)S(1)}, f32[128,1024]{1,0:T(8,128)S(1)}, u32[]{:S(2)}, u32[]{:S(2)}) collective-permute-start(f32[128,1024]{1,0:T(8,128)S(1)} %get-tuple-element.41), channel_id=1, source_target_pairs={{0,4},{4,0},{8,12},{12,8},{16,20},{20,16},{24,28},{28,24},{32,36},... | collective-permute-start | bytes 1572872 | tf_op jit(solution)/shard_map/ppermute | solution.py:368
  44.3 4.3 %copy-start = (f32[256,512]{1,0:T(8,128)}, f32[256,512]{1,0:T(8,128)S(1)}, u32[]{:S(2)}) copy-start(f32[256,512]{1,0:T(8,128)S(1)} %get-tuple-element.44.v) | copy-start | bytes 1572868
  60.8 17.7 %copy-start.2 = (f32[256,512]{1,0:T(8,128)}, f32[256,512]{1,0:T(8,128)S(1)}, u32[]{:S(2)}) copy-start(f32[256,512]{1,0:T(8,128)S(1)} %get-tuple-element.64.dq_part) | copy-start | bytes 1572868
  60.8 17.7 %copy-start.4 = (f32[256,512]{1,0:T(8,128)}, f32[256,512]{1,0:T(8,128)S(1)}, u32[]{:S(2)}) copy-start(f32[256,512]{1,0:T(8,128)S(1)} %get-tuple-element.61.g) | copy-start | bytes 1572868
  60.8 17.7 %copy-start.6 = (f32[256,512]{1,0:T(8,128)}, f32[256,512]{1,0:T(8,128)S(1)}, u32[]{:S(2)}) copy-start(f32[256,512]{1,0:T(8,128)S(1)} %get-tuple-element.62.hat) | copy-start | bytes 1572868
  60.8 5.7 %collective-permute-start.7 = (f32[256,1024]{1,0:T(8,128)S(1)}, f32[256,1024]{1,0:T(8,128)S(1)}, u32[]{:S(2)}, u32[]{:S(2)}) collective-permute-start(f32[256,1024]{1,0:T(8,128)S(1)} %get-tuple-element.71), channel_id=1, source_target_pairs={{0,4},{4,0},{8,12},{12,8},{16,20},{20,16},{24,28},{28,24},{32,36},... | collective-permute-start | bytes 3145736 | tf_op jit(solution)/shard_map/ppermute | solution.py:368
  66.6 11.8 %copy-start.16 = (f32[32,1024]{1,0:T(8,128)}, f32[32,1024]{1,0:T(8,128)S(1)}, u32[]{:S(2)}) copy-start(f32[32,1024]{1,0:T(8,128)S(1)} %get-tuple-element.74) | copy-start | bytes 393220
  66.7 11.8 %copy-start.18 = (f32[32,1024]{1,0:T(8,128)}, f32[32,1024]{1,0:T(8,128)S(1)}, u32[]{:S(2)}) copy-start(f32[32,1024]{1,0:T(8,128)S(1)} %get-tuple-element.73) | copy-start | bytes 393220
  66.7 12.6 %copy-start.14 = (f32[64,1024]{1,0:T(8,128)}, f32[64,1024]{1,0:T(8,128)S(1)}, u32[]{:S(2)}) copy-start(f32[64,1024]{1,0:T(8,128)S(1)} %get-tuple-element.72) | copy-start | bytes 786436
  66.7 16.2 %copy-start.13 = (f32[512]{0:T(512)S(1)}, f32[512]{0:T(512)}, u32[]{:S(2)}) copy-start(f32[512]{0:T(512)} %param.11) | copy-start | bytes 6148
  79.3 32.6 %all-to-all-start.3 = ((f32[4,16,1024]{2,1,0:T(8,128)}), f32[4,16,1024]{2,1,0:T(8,128)S(1)}, u32[]{:S(2)}, u32[]{:S(2)}) async-start(f32[4,16,1024]{2,1,0:T(8,128)} %shard_map.102), calls=%async_computation.3 | async-start | bytes 524288 | tf_op jit(solution)/shard_map/all_to_all | solution.py:371
  82.9 1.0 copy-start.1
  83.9 1.0 copy-start.3
  85.0 1.0 copy-start.5
  86.0 1.0 copy-start.7
  87.0 8.4 %copy-start.15 = (f32[64,1024]{1,0:T(8,128)S(1)}, f32[64,1024]{1,0:T(8,128)}, u32[]{:S(2)}) copy-start(f32[64,1024]{1,0:T(8,128)} %copy-done.14) | copy-start | bytes 786436
  87.0 10.7 %copy-start.19 = (f32[32,1024]{1,0:T(8,128)S(1)}, f32[32,1024]{1,0:T(8,128)}, u32[]{:S(2)}) copy-start(f32[32,1024]{1,0:T(8,128)} %copy-done.18) | copy-start | bytes 393220
  87.0 14.4 %copy-start.17 = (f32[32,1024]{1,0:T(8,128)S(1)}, f32[32,1024]{1,0:T(8,128)}, u32[]{:S(2)}) copy-start(f32[32,1024]{1,0:T(8,128)} %copy-done.16) | copy-start | bytes 393220
  90.2 0.8 copy-start.8
  91.0 0.8 copy-start.10
  91.8 13.3 %collective-permute-start.6 = (f32[128,1024]{1,0:T(8,128)S(1)}, f32[128,1024]{1,0:T(8,128)S(1)}, u32[]{:S(2)}, u32[]{:S(2)}) collective-permute-start(f32[128,1024]{1,0:T(8,128)S(1)} %get-tuple-element.69), channel_id=1, source_target_pairs={{0,4},{4,0},{8,12},{12,8},{16,20},{20,16},{24,28},{28,24},{32,36},... | collective-permute-start | bytes 1572872 | tf_op jit(solution)/shard_map/ppermute | solution.py:368
  95.5 16.4 %collective-permute-start.8 = (f32[64,1024]{1,0:T(8,128)S(1)}, f32[64,1024]{1,0:T(8,128)S(1)}, u32[]{:S(2)}, u32[]{:S(2)}) collective-permute-start(f32[64,1024]{1,0:T(8,128)S(1)} %copy-done.15), channel_id=1, source_target_pairs={{0,8},{4,12},{8,0},{12,4},{16,24},{20,28},{24,16},{28,20},{32,40},... | collective-permute-start | bytes 786440 | tf_op jit(solution)/shard_map/ppermute | solution.py:368
  97.7 10.9 %collective-permute-start.9 = (f32[32,1024]{1,0:T(8,128)S(1)}, f32[32,1024]{1,0:T(8,128)S(1)}, u32[]{:S(2)}, u32[]{:S(2)}) collective-permute-start(f32[32,1024]{1,0:T(8,128)S(1)} %copy-done.19), channel_id=1, source_target_pairs={{0,16},{4,20},{8,24},{12,28},{16,0},{20,4},{24,8},{28,12},{32,48},... | collective-permute-start | bytes 393224 | tf_op jit(solution)/shard_map/ppermute | solution.py:368
  101.4 10.4 %collective-permute-start.10 = (f32[32,1024]{1,0:T(8,128)S(1)}, f32[32,1024]{1,0:T(8,128)S(1)}, u32[]{:S(2)}, u32[]{:S(2)}) collective-permute-start(f32[32,1024]{1,0:T(8,128)S(1)} %copy-done.17), channel_id=1, source_target_pairs={{0,24},{4,28},{8,16},{12,20},{16,8},{20,12},{24,0},{28,4},{32,56},... | collective-permute-start | bytes 393224 | tf_op jit(solution)/shard_map/ppermute | solution.py:368
  111.8 1.0 copy-start.9
  112.9 1.0 copy-start.11
